TPU v7x, 256 devices: a whole 4x4x8 slice. The times are simulated.
256 devices in a mesh: tp: 2 (over z_lo), sp: 32 (over x, y, core), dp: 4 (over z_hi).
Axes of the slice: x: 4, y: 4, z: 8 (z_hi: 4, z_lo: 2; z = z_hi * 2 + z_lo), core: 2. Of those that a mesh axis runs over, the one named last changes fastest.
Arguments:
- queries: bfloat16 [16384, 4096], P(('dp', 'sp'), 'tp'), parts along dimension 0, may hold values from -256 to 256
- key_projection_rows: bfloat16 [16384, 512], P(('dp', 'sp'), 'tp'), parts along dimension 0, may hold values from -8 to 8
- values: bfloat16 [16384, 512], P(('dp', 'sp'), 'tp'), parts along dimension 0, may hold values from -6 to 6
- segment_ids: int32 [16384], P('dp'), parts along dimension 0, may hold values from 0 to 11, never falling along the last dimension, each value on 1 to 1024 neighbouring positions
- residual: bfloat16 [16384, 8192], P(('dp', 'tp'), 'sp'), parts along dimension 0, may hold values from -40 to 40
- out_weight: bfloat16 [4096, 8192], P('tp', 'sp'), may hold values from -0.09375 to 0.09375
- norm_gain: float32 [8192], P('sp'), may hold values from 0.1 to 1.9
- scale_exponent: int32 [8192], P('sp'), may hold values from 7 to 8
Outputs:
- hidden_out: bfloat16 [16384, 8192], P(('dp', 'tp'), 'sp'), parts along dimension 0
- quantized: bfloat16 [16384, 8192], P(('dp', 'tp'), 'sp'), parts along dimension 0
There are 4 independent parts, one for each index of `dp`. A program takes and returns all parts, laid end to end along the dimension named above; an argument that names none is the same for every part. Nothing has to cross between parts.
Inputs may be any that keep to these rules, and one draw needn't show every extreme that they name: `segment_ids`: never falls along the window; every document holds at most a quarter of the window's tokens, and one holds exactly that many.
All inputs are finite; a program needn't handle non-finite values.
Results may differ from a plain program's by a relative error of at most 0.0065.
Values may be sent and summed in bfloat16 or wider, within the bound.
No kernel may reach another device: no remote copies, remote signals or barrier semaphores. Data moves between devices by JAX's collectives and lax.ppermute only.
A program may use at most 64 MiB of HBM per device.

v0:
```python
import functools

import jax
import jax.numpy as jnp
from jax import lax
from jax.experimental import pallas as pl
from jax.experimental.pallas import tpu as pltpu
from jax.sharding import PartitionSpec as P


D = 8192
HEAD_DIMENSION = 128
GROUP_WIDTH = 8
LOG2E = 1.4426950408889634
SIZES = (64, 64)
LOWS = (0, 64)
CHUNKS = len(SIZES)
STACKED = 4

epsilon = 1e-05
limit_value = 448.0


def chip_shift(d):
    return [(s, ((s // 2 + d) % 16) * 2 + s % 2) for s in range(32)]


def core_swap():
    return [(s, s ^ 1) for s in range(32)]


def x_shift(d):
    return [(s, ((s // 8 + d) % 4) * 8 + s % 8) for s in range(32)]


def y_shift(d):
    return [(s, (s // 8) * 8 + ((s // 2 % 4 + d) % 4) * 2 + s % 2) for s in range(32)]


def send(value, perm):
    return lax.ppermute(value, "sp", perm)


VM = pl.BlockSpec(memory_space=pltpu.VMEM)


def near(*arrays):
    return [pltpu.with_memory_space_constraint(a, pltpu.VMEM) for a in arrays]


def limit(mib):
    return pltpu.CompilerParams(vmem_limit_bytes=mib << 20)


def place_of_device():
    s = lax.axis_index("sp")
    return s, s // 8, lax.rem(s // 2, 4), lax.rem(s, 2)


def join_kernel(k_ref, v_ref, o_ref, sem):
    width = k_ref.shape[1]
    copies = [
        pltpu.make_async_copy(ref, o_ref.at[:, pl.ds(i * width, width)], sem.at[i])
        for i, ref in enumerate((k_ref, v_ref))
    ]
    for copy in copies:
        copy.start()
    for copy in copies:
        copy.wait()


def join(k, v):
    return pl.pallas_call(
        join_kernel,
        out_shape=pltpu.VMEM((k.shape[0], 2 * k.shape[1]), k.dtype),
        in_specs=[pl.BlockSpec(memory_space=pl.ANY)] * 2,
        out_specs=VM,
        scratch_shapes=[pltpu.SemaphoreType.DMA((2,))],
        name="join",
    )(k, v)


def masks_kernel(seg_ref, q_ref, bias_a, bias_b, q_out):
    s = lax.axis_index("sp")
    hidden = jnp.float32(-1e30)
    own = jnp.broadcast_to(seg_ref[pl.ds(s, 1), :].astype(jnp.float32), (128, 128))
    query_seg = jnp.transpose(own)
    earlier = lax.broadcasted_iota(jnp.int32, (128, 128), 1) <= lax.broadcasted_iota(
        jnp.int32, (128, 128), 0
    )
    for block in range(9):
        row = s - 8 + block
        seg = seg_ref[pl.ds(jnp.maximum(row, 0), 1), :].astype(jnp.float32)
        seg = jnp.where(row >= 0, seg, jnp.float32(-1.0))
        seen = query_seg == seg
        if block == 8:
            seen = seen & earlier
        out = bias_b if block % 2 else bias_a
        low = block // 2 * 128
        out[:, low : low + 128] = jnp.where(seen, 0.0, hidden)
    q_out[...] = q_ref[...]


def masks(segments, q):
    return pl.pallas_call(
        masks_kernel,
        out_shape=(
            pltpu.VMEM((128, 640), jnp.float32),
            pltpu.VMEM((128, 512), jnp.float32),
            pltpu.VMEM(q.shape, q.dtype),
        ),
        in_specs=[VM, VM],
        out_specs=(VM, VM, VM),
        compiler_params=limit(6),
        name="masks",
    )(segments, q)


def keys_kernel(*refs):
    blocks, all_ref, give_ref = refs[:-2], refs[-2], refs[-1]
    core = lax.rem(lax.axis_index("sp"), 2)
    rows = blocks[0].shape[0]
    for number, block in enumerate(blocks):
        all_ref[number * rows : (number + 1) * rows, :] = block[...]
    give_ref[...] = all_ref[pl.ds(pl.multiple_of((1 - core) * rows, rows), give_ref.shape[0]), :]


def stack_keys(blocks):
    rows, width = blocks[0].shape
    count = len(blocks)
    return pl.pallas_call(
        keys_kernel,
        out_shape=(
            pltpu.VMEM((count * rows, width), blocks[0].dtype),
            pltpu.VMEM(((count - 1) * rows, width), blocks[0].dtype),
        ),
        in_specs=[VM] * count,
        out_specs=(VM, VM),
        compiler_params=limit(4),
        name="stack_keys",
    )(*near(*blocks))


def attention_kernel(q_ref, a_ref, b_ref, bias_a, bias_b, *outs):
    rows = q_ref.shape[0]
    na, nb = a_ref.shape[0], b_ref.shape[0]
    factor = jnp.float32(LOG2E * HEAD_DIMENSION**-0.5)
    groups = a_ref.shape[1] // (2 * HEAD_DIMENSION)
    contract = (((1,), (1,)), ((), ()))
    for group in range(groups):
        kcols = slice(group * 128, (group + 1) * 128)
        vcols = slice((groups + group) * 128, (groups + group + 1) * 128)
        ka, kb = a_ref[:, kcols], b_ref[:, kcols]
        va = jnp.concatenate([a_ref[:, vcols], jnp.ones((na, 128), jnp.bfloat16)], axis=1)
        vb = jnp.concatenate([b_ref[:, vcols], jnp.ones((nb, 128), jnp.bfloat16)], axis=1)
        for first in range(0, GROUP_WIDTH, STACKED):
            heads = [group * GROUP_WIDTH + first + i for i in range(STACKED)]
            q = jnp.concatenate([q_ref[:, h * 128 : (h + 1) * 128] for h in heads], axis=0)
            mask_a = jnp.concatenate([bias_a[...]] * STACKED, axis=0)
            mask_b = jnp.concatenate([bias_b[...]] * STACKED, axis=0)
            sa = lax.dot_general(q, ka, contract, preferred_element_type=jnp.float32) + mask_a
            sb = lax.dot_general(q, kb, contract, preferred_element_type=jnp.float32) + mask_b
            top = jnp.maximum(jnp.max(sa, axis=1, keepdims=True), jnp.max(sb, axis=1, keepdims=True))
            pa = jnp.exp2((sa - top) * factor).astype(jnp.bfloat16)
            pb = jnp.exp2((sb - top) * factor).astype(jnp.bfloat16)
            out = jnp.dot(pa, va, preferred_element_type=jnp.float32) + jnp.dot(
                pb, vb, preferred_element_type=jnp.float32
            )
            done = (out[:, :128] / out[:, 128:]).astype(jnp.bfloat16)
            for i, h in enumerate(heads):
                for low, size, out_ref in zip(LOWS, SIZES, outs):
                    at = i * rows + low
                    out_ref[:, h * 128 : (h + 1) * 128] = done[at : at + size]


def attend(q, keys_a, keys_b, bias_a, bias_b):
    rows, width = q.shape
    return pl.pallas_call(
        attention_kernel,
        out_shape=tuple(pltpu.VMEM((size, width), jnp.bfloat16) for size in SIZES),
        in_specs=[VM] * 5,
        out_specs=tuple([VM] * CHUNKS),
        cost_estimate=pl.CostEstimate(
            flops=rows * width * 1152 * 6, bytes_accessed=3 << 20, transcendentals=rows * 16 * 1152
        ),
        compiler_params=limit(16),
        name="attend",
    )(*near(q, keys_a, keys_b, bias_a, bias_b))


def project_kernel(sets, splits, *refs):
    parts, weights = refs[: 4 * sets], list(refs[4 * sets : -3])
    give_ref, keep_ref, lhs = refs[-3:]
    _, x, _, _ = place_of_device()
    tp = lax.axis_index("tp")
    sizes = [parts[4 * i].shape[0] for i in range(sets)]
    half = 2 * sum(sizes)
    for r in range(4):
        owner = lax.rem(x + 4 - r, 4)
        side = jnp.where(owner // 2 == tp, half, 0)
        for i, size in enumerate(sizes):
            start = side + 2 * sum(sizes[:i]) + lax.rem(owner, 2) * size
            lhs[pl.ds(pl.multiple_of(start, 16), size), :] = parts[4 * i + r][...]
    for number, split in enumerate(splits):
        pieces = [weights.pop(0) for _ in range(split)]
        depth, width = pieces[0].shape
        cols = slice(number * width, (number + 1) * width)
        total = sum(
            jnp.dot(lhs[:, k * depth : (k + 1) * depth], piece[...], preferred_element_type=jnp.float32)
            for k, piece in enumerate(pieces)
        )
        give_ref[:, cols] = total[:half].astype(jnp.bfloat16)
        keep_ref[:, cols] = total[half:]


def project(parts, groups):
    depth = parts[0].shape[1]
    sets = len(parts) // 4
    half = 2 * sum(part.shape[0] for part in parts[::4])
    width = sum(pieces[0].shape[1] for pieces in groups)
    weights = [piece for pieces in groups for piece in pieces]
    splits = tuple(len(pieces) for pieces in groups)
    return pl.pallas_call(
        functools.partial(project_kernel, sets, splits),
        out_shape=(
            pltpu.VMEM((half, width), jnp.bfloat16),
            pltpu.VMEM((half, width), jnp.float32),
        ),
        in_specs=[VM] * (len(parts) + len(weights)),
        out_specs=(VM, VM),
        scratch_shapes=[pltpu.VMEM((2 * half, depth), jnp.bfloat16)],
        cost_estimate=pl.CostEstimate(
            flops=4 * half * depth * width, bytes_accessed=8 << 20, transcendentals=0
        ),
        compiler_params=limit(14),
        name="project",
    )(*near(*parts, *weights))


def combine_kernel(keep_ref, got_ref, *pieces):
    width = pieces[0].shape[-1]
    for number, piece in enumerate(pieces):
        for k in range(2):
            cols = slice((2 * number + k) * width, (2 * number + k + 1) * width)
            piece[k] = (keep_ref[:, cols] + got_ref[:, cols].astype(jnp.float32)).astype(jnp.bfloat16)


def combine(keep, got):
    total, width = keep.shape
    count = width // 512
    return pl.pallas_call(
        combine_kernel,
        out_shape=tuple([pltpu.VMEM((2, total, 256), jnp.bfloat16)] * count),
        in_specs=[VM] * 2,
        out_specs=tuple([VM] * count),
        compiler_params=limit(6),
        name="combine",
    )(*near(keep, got))


def pack_kernel(*refs):
    out, low = refs[-1], 0
    for piece in refs[:-1]:
        size = piece.shape[1]
        out[low : low + size, :] = piece[1]
        low += size


def pack(pieces):
    width = pieces[0].shape[-1]
    total = sum(p.shape[1] for p in pieces)
    return pl.pallas_call(
        pack_kernel,
        out_shape=pltpu.VMEM((total, width), jnp.bfloat16),
        in_specs=[VM] * len(pieces),
        out_specs=VM,
        compiler_params=limit(4),
        name="pack",
    )(*near(*pieces))


def place_kernel(plan, count, residual_ref, gain_ref, exponent_ref, *refs):
    near_refs, far_refs = refs[:count], refs[count:-3]
    out, copy, table = refs[-3:]
    table[:1] = gain_ref[...]
    table[1:2] = limit_value * jnp.exp2(-exponent_ref[...].astype(jnp.float32))
    _, _, y, core = place_of_device()

    def put(start, piece):
        at = pl.ds(pl.multiple_of(start, 16), piece.shape[0])
        out[at, :] = (residual_ref[at, :].astype(jnp.float32) + piece.astype(jnp.float32)).astype(
            jnp.bfloat16
        )

    for r, chunk, source, source_low, packed, packed_low in plan:
        for i in range(2):
            rows = SIZES[chunk]
            base = i * 1024 + lax.rem(y + r, 4) * 256 + LOWS[chunk]
            low = source_low + i * rows
            put(base + core * 128, near_refs[source][0, low : low + rows, :])
            low = packed_low + i * rows
            put(base + (1 - core) * 128, far_refs[packed][low : low + rows, :])
    copy[...] = out[...]


def place(residual, gain, exponent, plan, near_parts, far_parts):
    width = residual.shape[1]
    return pl.pallas_call(
        functools.partial(place_kernel, plan, len(near_parts)),
        out_shape=(
            pltpu.VMEM(residual.shape, jnp.bfloat16),
            jax.ShapeDtypeStruct(residual.shape, jnp.bfloat16),
            pltpu.VMEM((8, width), jnp.float32),
        ),
        in_specs=[VM] * (3 + len(near_parts) + len(far_parts)),
        out_specs=(VM, VM, VM),
        compiler_params=limit(6),
        name="place",
    )(residual, gain.reshape(1, width), exponent.reshape(1, width), *near(*near_parts, *far_parts))


def spread_kernel(residual_ref, *outs):
    _, _, y, _ = place_of_device()
    for r, out in enumerate(outs):
        for i in range(2):
            start = pl.multiple_of(i * 1024 + lax.rem(y + r, 4) * 256, 256)
            out[i] = residual_ref[pl.ds(start, 256), :]


def spread(residual):
    width = residual.shape[1]
    return pl.pallas_call(
        spread_kernel,
        out_shape=tuple([pltpu.VMEM((2, 256, width), jnp.bfloat16)] * 4),
        in_specs=[VM],
        out_specs=tuple([VM] * 4),
        compiler_params=limit(4),
        name="spread",
    )(residual)


def trade_kernel(*refs):
    core = lax.rem(lax.axis_index("sp"), 2)
    start = pl.multiple_of((1 - core) * 128, 128)
    for r, line in enumerate(refs[:-1]):
        for i in range(2):
            refs[-1][r, i] = line[i, pl.ds(start, 128), :]


def trade(lines):
    width = lines[0].shape[-1]
    return pl.pallas_call(
        trade_kernel,
        out_shape=pltpu.VMEM((4, 2, 128, width), jnp.bfloat16),
        in_specs=[VM] * 4,
        out_specs=VM,
        compiler_params=limit(4),
        name="trade",
    )(*near(*lines))


def squares_kernel(*refs):
    pieces, lines, far_ref, out = refs[:7], refs[7:11], refs[11], refs[12]
    core = lax.rem(lax.axis_index("sp"), 2)
    own, down, up, last = pieces[0:2], pieces[2:4], pieces[4:6], pieces[6]
    sums = []
    for i in range(2):
        halves = []
        for chunk in range(CHUNKS):
            rows, low = SIZES[chunk], LOWS[chunk]
            total = jnp.zeros((rows, 256), jnp.float32)
            sources = (
                (own[chunk], i * rows),
                (down[chunk], i * rows),
                (last, 2 * low + i * rows),
                (up[chunk], i * rows),
            )
            for r, (piece, at) in enumerate(sources):
                start = pl.multiple_of(core * 128 + low, 16)
                for k, res in enumerate(
                    (lines[r][i, pl.ds(start, rows), :], far_ref[r, i, low : low + rows, :])
                ):
                    added = res.astype(jnp.float32) + piece[k, at : at + rows, :].astype(jnp.float32)
                    wide = added.astype(jnp.bfloat16).astype(jnp.float32)
                    total = total + wide * wide
            halves.append(total)
        block = jnp.sum(jnp.concatenate(halves, axis=0), axis=1, keepdims=True)
        sums.append(jnp.transpose(jnp.broadcast_to(block, (128, 128)))[:1])
    line = jnp.concatenate(sums, axis=1)
    out[...] = jnp.broadcast_to(line[None], out.shape)


def squares_of(pieces, lines, far):
    return pl.pallas_call(
        squares_kernel,
        out_shape=pltpu.VMEM((32, 1, 256), jnp.float32),
        in_specs=[VM] * 12,
        out_specs=VM,
        compiler_params=limit(6),
        name="squares",
    )(*near(*pieces, *lines, far))


def finish_kernel(hidden_ref, sums_ref, table_ref, quantized_out):
    step = pl.program_id(0)
    rows = quantized_out.shape[0]
    gain, bound = table_ref[:1], table_ref[1:2]
    for block in range(rows // 128):
        start = pl.multiple_of(step * rows + block * 128, 128)
        number = step * (rows // 128) + block
        lane = pl.ds(pl.multiple_of(number // 8 * 128, 128), 128)
        total = sum(sums_ref[lax.rem(number, 8) + 8 * x, :, lane] for x in range(4))
        scale = lax.rsqrt(total / D + epsilon)
        column = jnp.transpose(jnp.broadcast_to(scale, (128, 128)))
        hidden = hidden_ref[pl.ds(start, 128), :]
        at = slice(block * 128, (block + 1) * 128)
        wide = hidden.astype(jnp.float32)
        normed = wide * jnp.concatenate([column, column], axis=1) * gain
        quantized_out[at, :] = jnp.clip(normed, -bound, bound).astype(jnp.bfloat16)


def finish(hidden, sums, table):
    tokens, width = hidden.shape
    steps = 2
    block = pl.BlockSpec((tokens // steps, width), lambda i: (i, 0))
    return pl.pallas_call(
        finish_kernel,
        grid=(steps,),
        out_shape=jax.ShapeDtypeStruct(hidden.shape, jnp.bfloat16),
        in_specs=[VM, VM, VM],
        out_specs=block,
        compiler_params=limit(8),
        name="finish",
    )(hidden, sums, table)


def inner(
    queries,
    key_projection_rows,
    values,
    segment_ids,
    residual,
    out_weight,
    norm_gain,
    scale_exponent,
):
    (residual,) = near(residual)
    own_kv = join(key_projection_rows, values)
    early = [send(own_kv, chip_shift(d)) for d in (4, 3, 2, 1)]
    bias_a, bias_b, q = masks(segment_ids.reshape(32, 128), queries)
    keys_a, leave = stack_keys(early + [own_kv])
    keys_b = send(leave, core_swap())

    half = out_weight.shape[0] // 2
    top, bottom = out_weight[:half], out_weight[half:]
    down_top, up_bottom = send(top, y_shift(1)), send(bottom, y_shift(-1))
    down_bottom, up_top = send(bottom, y_shift(1)), send(top, y_shift(-1))
    far = (send(down_top, y_shift(1)), send(up_bottom, y_shift(-1)))

    def both(pieces):
        return [pieces, tuple(send(w, core_swap()) for w in pieces)]

    near_weights = both((out_weight,)) + both((down_top, down_bottom)) + both((up_top, up_bottom))
    far_weights = both(far)

    att = attend(q, keys_a, keys_b, bias_a, bias_b)
    lines = [
        [att[chunk]] + [send(att[chunk], x_shift(d)) for d in (1, 2, 3)]
        for chunk in range(CHUNKS)
    ]

    def across(parts, weights):
        give, keep = project(parts, weights)
        got = lax.ppermute(give, "tp", [(0, 1), (1, 0)])
        return combine(keep, got)

    lines_out = spread(residual)
    res = [piece if r == 0 else send(piece, y_shift(r)) for r, piece in enumerate(lines_out)]
    traded = trade(res)
    res_far = send(traded, core_swap())

    made, own, down, up = [], [], [], []
    for chunk in range(CHUNKS):
        if chunk == 0:
            pieces = [*across(lines[0], near_weights[:2]), *across(lines[0], near_weights[2:])]
        else:
            pieces = across(lines[chunk], near_weights)
        made.append(pieces)
        own.append(pieces[0])
        down.append(send(pieces[1], y_shift(-1)))
        up.append(send(pieces[2], y_shift(1)))
    (piece,) = across(lines[0] + lines[1], far_weights)
    last = send(piece, y_shift(2))
    squares = squares_of([made[c][g] for g in range(3) for c in range(2)] + [piece], res, res_far)
    sums = lax.all_to_all(squares, "sp", 0, 0, tiled=True)
    batches = [
        [(0, (0,), own[0]), (0, (1,), own[1]), (1, (0,), down[0]), (3, (0,), up[0])],
        [(1, (1,), down[1]), (3, (1,), up[1]), (2, (0, 1), last)],
    ]
    near_parts, far_parts, plan = [], [], []
    for number, batch in enumerate(batches):
        low = 0
        for r, chunks, part in batch:
            for chunk in chunks:
                source_low = 2 * LOWS[chunk] if len(chunks) > 1 else 0
                plan.append((r, chunk, len(near_parts), source_low, number, low))
                low += 2 * SIZES[chunk]
            near_parts.append(part)
        packed = pack([part for _, _, part in batch])
        far_parts.append(send(packed, core_swap()))
    hidden, hidden_out, table = place(
        residual, norm_gain, scale_exponent, tuple(plan), near_parts, far_parts
    )
    return hidden_out, finish(hidden, sums, table)


def solution(mesh):
    in_specs = (
        P(("dp", "sp"), "tp"),
        P(("dp", "sp"), "tp"),
        P(("dp", "sp"), "tp"),
        P("dp"),
        P(("dp", "tp"), "sp"),
        P("tp", "sp"),
        P("sp"),
        P("sp"),
    )
    out_specs = (P(("dp", "tp"), "sp"), P(("dp", "tp"), "sp"))
    return jax.shard_map(inner, mesh=mesh, in_specs=in_specs, out_specs=out_specs, check_vma=False)
```

profile of v0, /device:TPU:1, one launch (start us, length us, event | category | flops | bytes accessed | tf_op | source)
XLA Modules:
  0.0 144.7 jit_solution(10032652141478116923)
XLA Ops:
  1.5 2.1 %collective-permute-start = (bf16[128,512]{1,0:T(8,128)(2,1)S(1)}, bf16[128,512]{1,0:T(8,128)(2,1)S(1)}, u32[]{:S(2)}, u32[]{:S(2)}) collective-permute-start(bf16[128,512]{1,0:T(8,128)(2,1)S(1)} %join.1.refs_4_), channel_id=1, source_target_pairs={{0,32},{4,36},{8,40},{12,44},{16,48},{20,52},{24,56},{28,60},{32,6... | collective-permute-start | bytes 393224 | tf_op jit(solution)/shard_map/ppermute | solution.py:41
  3.6 2.7 %collective-permute-start.1 = (bf16[128,512]{1,0:T(8,128)(2,1)S(1)}, bf16[128,512]{1,0:T(8,128)(2,1)S(1)}, u32[]{:S(2)}, u32[]{:S(2)}) collective-permute-start(bf16[128,512]{1,0:T(8,128)(2,1)S(1)} %join.1.refs_4_), channel_id=1, source_target_pairs={{0,24},{4,28},{8,32},{12,36},{16,40},{20,44},{24,48},{28,52},{32,5... | collective-permute-start | bytes 393224 | tf_op jit(solution)/shard_map/ppermute | solution.py:41
  6.4 1.3 collective-permute-start.2
  8.3 3.5 %collective-permute-done.1.refs_1_ = bf16[128,512]{1,0:T(8,128)(2,1)S(1)} collective-permute-done((bf16[128,512]{1,0:T(8,128)(2,1)S(1)}, bf16[128,512]{1,0:T(8,128)(2,1)S(1)}, u32[]{:S(2)}, u32[]{:S(2)}) %collective-permute-start.1) | collective-permute-done | bytes 131104 | tf_op jit(solution)/shard_map/ppermute | solution.py:41
  11.8 4.4 %collective-permute-done.2.refs_2_ = bf16[128,512]{1,0:T(8,128)(2,1)S(1)} collective-permute-done((bf16[128,512]{1,0:T(8,128)(2,1)S(1)}, bf16[128,512]{1,0:T(8,128)(2,1)S(1)}, u32[]{:S(2)}, u32[]{:S(2)}) %collective-permute-start.2) | collective-permute-done | bytes 131104 | tf_op jit(solution)/shard_map/ppermute | solution.py:41
  16.3 2.6 %collective-permute-done.3.refs_3_ = bf16[128,512]{1,0:T(8,128)(2,1)S(1)} collective-permute-done((bf16[128,512]{1,0:T(8,128)(2,1)S(1)}, bf16[128,512]{1,0:T(8,128)(2,1)S(1)}, u32[]{:S(2)}, u32[]{:S(2)}) %collective-permute-start.3) | collective-permute-done | bytes 131104 | tf_op jit(solution)/shard_map/ppermute | solution.py:41
  19.0 1.9 %collective-permute-start.4 = (bf16[512,512]{1,0:T(8,128)(2,1)S(1)}, bf16[512,512]{1,0:T(8,128)(2,1)S(1)}, u32[]{:S(2)}, u32[]{:S(2)}) collective-permute-start(bf16[512,512]{1,0:T(8,128)(2,1)S(1)} %get-tuple-element.31), channel_id=1, source_target_pairs={{0,4},{4,0},{8,12},{12,8},{16,20},{20,16},{24,28},{28,24},{32,36},... | collective-permute-start | bytes 1572872 | tf_op jit(solution)/shard_map/ppermute | solution.py:41
  20.9 1.3 fusion
  22.4 2.7 %collective-permute-start.17 = (bf16[1024,256]{1,0:T(8,128)(2,1)S(1)}, bf16[1024,256]{1,0:T(8,128)(2,1)S(1)}, u32[]{:S(2)}, u32[]{:S(2)}) collective-permute-start(bf16[1024,256]{1,0:T(8,128)(2,1)S(1)} %get-tuple-element.57), channel_id=1, source_target_pairs={{0,24},{4,28},{8,0},{12,4},{16,8},{20,12},{24,16},{28,20},{32,56},... | collective-permute-start | bytes 1572872 | tf_op jit(solution)/shard_map/ppermute | solution.py:41
  25.0 1.4 collective-permute-start.18
  26.6 3.3 %attend.1 = (bf16[64,2048]{1,0:T(8,128)(2,1)S(1)}, bf16[64,2048]{1,0:T(8,128)(2,1)S(1)}) custom-call(bf16[128,2048]{1,0:T(8,128)(2,1)S(1)} %get-tuple-element.29.q_ref, bf16[640,512]{1,0:T(8,128)(2,1)S(1)} %get-tuple-element.30.a_ref, bf16[512,512]{1,0:T(8,128)(2,1)S(1)} %collective-permute-done.4.b_ref, f32[128,640]{1,0:T(8,128)S(1)} %get-tuple-element.32.bias_a, ...), custom_call_target="tpu_custom_call" | custom-call | flops 1811939328 | bytes 3145728 | tf_op jit(solution)/shard_map/attend/pallas_call | solution.py:178
  30.0 6.9 %collective-permute-done.13.refs_6_.refs_4_ = bf16[1024,256]{1,0:T(8,128)(2,1)S(1)} collective-permute-done((bf16[1024,256]{1,0:T(8,128)(2,1)S(1)}, bf16[1024,256]{1,0:T(8,128)(2,1)S(1)}, u32[]{:S(2)}, u32[]{:S(2)}) %collective-permute-start.13) | collective-permute-done | bytes 524320 | tf_op jit(solution)/shard_map/ppermute | solution.py:41
  36.9 1.5 %collective-permute-start.6 = (bf16[64,2048]{1,0:T(8,128)(2,1)S(1)}, bf16[64,2048]{1,0:T(8,128)(2,1)S(1)}, u32[]{:S(2)}, u32[]{:S(2)}) collective-permute-start(bf16[64,2048]{1,0:T(8,128)(2,1)S(1)} %get-tuple-element.34.refs_0_), channel_id=1, source_target_pairs={{0,64},{4,68},{8,72},{12,76},{16,80},{20,84},{24,88},{28,92},{32,9... | collective-permute-start | bytes 786440 | tf_op jit(solution)/shard_map/ppermute | solution.py:41
  38.4 9.7 %collective-permute-done.14.refs_7_.refs_5_ = bf16[1024,256]{1,0:T(8,128)(2,1)S(1)} collective-permute-done((bf16[1024,256]{1,0:T(8,128)(2,1)S(1)}, bf16[1024,256]{1,0:T(8,128)(2,1)S(1)}, u32[]{:S(2)}, u32[]{:S(2)}) %collective-permute-start.14) | collective-permute-done | bytes 524320 | tf_op jit(solution)/shard_map/ppermute | solution.py:41
  48.1 0.9 collective-permute-start.15
  49.0 1.3 collective-permute-start.7
  50.5 1.5 %collective-permute-start.11 = (bf16[64,2048]{1,0:T(8,128)(2,1)S(1)}, bf16[64,2048]{1,0:T(8,128)(2,1)S(1)}, u32[]{:S(2)}, u32[]{:S(2)}) collective-permute-start(bf16[64,2048]{1,0:T(8,128)(2,1)S(1)} %get-tuple-element.37.refs_0_.refs_4_), channel_id=1, source_target_pairs={{0,64},{4,68},{8,72},{12,76},{16,80},{20,84},{24,88},{28,92},{32,9... | collective-permute-start | bytes 786440 | tf_op jit(solution)/shard_map/ppermute | solution.py:41
  52.9 4.0 %collective-permute-done.7.refs_3_ = bf16[64,2048]{1,0:T(8,128)(2,1)S(1)} collective-permute-done((bf16[64,2048]{1,0:T(8,128)(2,1)S(1)}, bf16[64,2048]{1,0:T(8,128)(2,1)S(1)}, u32[]{:S(2)}, u32[]{:S(2)}) %collective-permute-start.7) | collective-permute-done | bytes 262176 | tf_op jit(solution)/shard_map/ppermute | solution.py:41
  56.9 1.3 collective-permute-start.8
  58.2 6.5 %collective-permute-done.10.refs_1_.refs_5_ = bf16[64,2048]{1,0:T(8,128)(2,1)S(1)} collective-permute-done((bf16[64,2048]{1,0:T(8,128)(2,1)S(1)}, bf16[64,2048]{1,0:T(8,128)(2,1)S(1)}, u32[]{:S(2)}, u32[]{:S(2)}) %collective-permute-start.10) | collective-permute-done | bytes 262176 | tf_op jit(solution)/shard_map/ppermute | solution.py:41
  64.7 2.7 %collective-permute-start.28 = (bf16[1024,256]{1,0:T(8,128)(2,1)S(1)}, bf16[1024,256]{1,0:T(8,128)(2,1)S(1)}, u32[]{:S(2)}, u32[]{:S(2)}) collective-permute-start(bf16[1024,256]{1,0:T(8,128)(2,1)S(1)} %collective-permute-done.18.refs_11_.refs_9_), channel_id=1, source_target_pairs={{0,24},{4,28},{8,0},{12,4},{16,8},{20,12},{24,16},{28,20},{32,56},... | collective-permute-start | bytes 1572872 | tf_op jit(solution)/shard_map/ppermute | solution.py:41
  67.4 1.7 %collective-permute-start.19 = (bf16[1024,256]{1,0:T(8,128)(2,1)S(1)}, bf16[1024,256]{1,0:T(8,128)(2,1)S(1)}, u32[]{:S(2)}, u32[]{:S(2)}) collective-permute-start(bf16[1024,256]{1,0:T(8,128)(2,1)S(1)} %collective-permute-done.17.refs_10_.refs_8_), channel_id=1, source_target_pairs={{0,4},{4,0},{8,12},{12,8},{16,20},{20,16},{24,28},{28,24},{32,36},... | collective-permute-start | bytes 1572872 | tf_op jit(solution)/shard_map/ppermute | solution.py:41
  69.2 9.1 %collective-permute-done.27.refs_8_ = bf16[1024,256]{1,0:T(8,128)(2,1)S(1)} collective-permute-done((bf16[1024,256]{1,0:T(8,128)(2,1)S(1)}, bf16[1024,256]{1,0:T(8,128)(2,1)S(1)}, u32[]{:S(2)}, u32[]{:S(2)}) %collective-permute-start.27) | collective-permute-done | bytes 524320 | tf_op jit(solution)/shard_map/ppermute | solution.py:41
  78.3 2.0 %collective-permute-start.29 = (bf16[1024,256]{1,0:T(8,128)(2,1)S(1)}, bf16[1024,256]{1,0:T(8,128)(2,1)S(1)}, u32[]{:S(2)}, u32[]{:S(2)}) collective-permute-start(bf16[1024,256]{1,0:T(8,128)(2,1)S(1)} %collective-permute-done.27.refs_8_), channel_id=1, source_target_pairs={{0,4},{4,0},{8,12},{12,8},{16,20},{20,16},{24,28},{28,24},{32,36},... | collective-permute-start | bytes 1572872 | tf_op jit(solution)/shard_map/ppermute | solution.py:41
  80.6 1.3 project.6
  81.9 5.9 %collective-permute-done.12.refs_3_.refs_7_ = bf16[64,2048]{1,0:T(8,128)(2,1)S(1)} collective-permute-done((bf16[64,2048]{1,0:T(8,128)(2,1)S(1)}, bf16[64,2048]{1,0:T(8,128)(2,1)S(1)}, u32[]{:S(2)}, u32[]{:S(2)}) %collective-permute-start.12) | collective-permute-done | bytes 262176 | tf_op jit(solution)/shard_map/ppermute | solution.py:41
  87.8 1.5 %collective-permute-start.36 = (bf16[2,256,256]{2,1,0:T(8,128)(2,1)S(1)}, bf16[2,256,256]{2,1,0:T(8,128)(2,1)S(1)}, u32[]{:S(2)}, u32[]{:S(2)}) collective-permute-start(bf16[2,256,256]{2,1,0:T(8,128)(2,1)S(1)} %get-tuple-element.53), channel_id=1, source_target_pairs={{0,16},{4,20},{8,24},{12,28},{16,0},{20,4},{24,8},{28,12},{32,48},... | collective-permute-start | bytes 786440 | tf_op jit(solution)/shard_map/ppermute | solution.py:41
  89.3 1.5 %collective-permute-start.37 = (bf16[2,256,256]{2,1,0:T(8,128)(2,1)S(1)}, bf16[2,256,256]{2,1,0:T(8,128)(2,1)S(1)}, u32[]{:S(2)}, u32[]{:S(2)}) collective-permute-start(bf16[2,256,256]{2,1,0:T(8,128)(2,1)S(1)} %get-tuple-element.54), channel_id=1, source_target_pairs={{0,24},{4,28},{8,0},{12,4},{16,8},{20,12},{24,16},{28,20},{32,56},... | collective-permute-start | bytes 786440 | tf_op jit(solution)/shard_map/ppermute | solution.py:41
  90.8 1.8 %project.5 = (bf16[128,1536]{1,0:T(8,128)(2,1)S(1)}, f32[128,1536]{1,0:T(8,128)S(1)}) custom-call(bf16[64,2048]{1,0:T(8,128)(2,1)S(1)} %get-tuple-element.37.refs_0_.refs_4_, bf16[64,2048]{1,0:T(8,128)(2,1)S(1)} %collective-permute-done.10.refs_1_.refs_5_, bf16[64,2048]{1,0:T(8,128)(2,1)S(1)} %collective-permute-done.11.refs_2_.refs_6_, ...), custom_call_target="tpu_custom_call" | custom-call | flops 1610612736 | bytes 8388608 | tf_op jit(solution)/shard_map/project/pallas_call | solution.py:223
  92.7 1.9 %collective-permute-start.21 = (bf16[128,1536]{1,0:T(8,128)(2,1)S(1)}, bf16[128,1536]{1,0:T(8,128)(2,1)S(1)}, u32[]{:S(2)}, u32[]{:S(2)}) collective-permute-start(bf16[128,1536]{1,0:T(8,128)(2,1)S(1)} %get-tuple-element.39), channel_id=1, source_target_pairs={{0,128},{128,0},{1,129},{129,1},{2,130},{130,2},{3,131},{131,3},{4... | collective-permute-start | bytes 1179656 | tf_op jit(solution)/shard_map/ppermute | solution.py:474
  94.7 1.4 project.7
  96.1 1.4 collective-permute-start.31
  97.6 5.1 %collective-permute-done.37.refs_3_.refs_10_ = bf16[2,256,256]{2,1,0:T(8,128)(2,1)S(1)} collective-permute-done((bf16[2,256,256]{2,1,0:T(8,128)(2,1)S(1)}, bf16[2,256,256]{2,1,0:T(8,128)(2,1)S(1)}, u32[]{:S(2)}, u32[]{:S(2)}) %collective-permute-start.37) | collective-permute-done | bytes 262176 | tf_op jit(solution)/shard_map/ppermute | solution.py:41
  102.7 1.8 %collective-permute-start.38 = (bf16[4,2,128,256]{3,2,1,0:T(8,128)(2,1)S(1)}, bf16[4,2,128,256]{3,2,1,0:T(8,128)(2,1)S(1)}, u32[]{:S(2)}, u32[]{:S(2)}) collective-permute-start(bf16[4,2,128,256]{3,2,1,0:T(8,128)(2,1)S(1)} %trade.1), channel_id=1, source_target_pairs={{0,4},{4,0},{8,12},{12,8},{16,20},{20,16},{24,28},{28,24},{32,36},... | collective-permute-start | bytes 1572872 | tf_op jit(solution)/shard_map/ppermute | solution.py:41
  105.2 1.7 %collective-permute-start.9 = (bf16[128,512]{1,0:T(8,128)(2,1)S(1)}, bf16[128,512]{1,0:T(8,128)(2,1)S(1)}, u32[]{:S(2)}, u32[]{:S(2)}) collective-permute-start(bf16[128,512]{1,0:T(8,128)(2,1)S(1)} %get-tuple-element.36), channel_id=1, source_target_pairs={{0,128},{128,0},{1,129},{129,1},{2,130},{130,2},{3,131},{131,3},{4... | collective-permute-start | bytes 393224 | tf_op jit(solution)/shard_map/ppermute | solution.py:474
  106.9 1.6 %collective-permute-done.22.got_ref = bf16[128,1024]{1,0:T(8,128)(2,1)S(1)} collective-permute-done((bf16[128,1024]{1,0:T(8,128)(2,1)S(1)}, bf16[128,1024]{1,0:T(8,128)(2,1)S(1)}, u32[]{:S(2)}, u32[]{:S(2)}) %collective-permute-start.22) | collective-permute-done | bytes 262176 | tf_op jit(solution)/shard_map/ppermute | solution.py:474
  109.1 5.0 %collective-permute-done.31.got_ref = bf16[256,512]{1,0:T(8,128)(2,1)S(1)} collective-permute-done((bf16[256,512]{1,0:T(8,128)(2,1)S(1)}, bf16[256,512]{1,0:T(8,128)(2,1)S(1)}, u32[]{:S(2)}, u32[]{:S(2)}) %collective-permute-start.31) | collective-permute-done | bytes 262176 | tf_op jit(solution)/shard_map/ppermute | solution.py:474
  114.1 2.2 %collective-permute-start.32 = (bf16[2,256,256]{2,1,0:T(8,128)(2,1)S(1)}, bf16[2,256,256]{2,1,0:T(8,128)(2,1)S(1)}, u32[]{:S(2)}, u32[]{:S(2)}) collective-permute-start(bf16[2,256,256]{2,1,0:T(8,128)(2,1)S(1)} %combine.7.refs_6_), channel_id=1, source_target_pairs={{0,16},{4,20},{8,24},{12,28},{16,0},{20,4},{24,8},{28,12},{32,48},... | collective-permute-start | bytes 786440 | tf_op jit(solution)/shard_map/ppermute | solution.py:41
  116.9 2.2 %collective-permute-start.25 = (bf16[2,128,256]{2,1,0:T(8,128)(2,1)S(1)}, bf16[2,128,256]{2,1,0:T(8,128)(2,1)S(1)}, u32[]{:S(2)}, u32[]{:S(2)}) collective-permute-start(bf16[2,128,256]{2,1,0:T(8,128)(2,1)S(1)} %get-tuple-element.45.refs_3_), channel_id=1, source_target_pairs={{0,24},{4,28},{8,0},{12,4},{16,8},{20,12},{24,16},{28,20},{32,56},... | collective-permute-start | bytes 393224 | tf_op jit(solution)/shard_map/ppermute | solution.py:41
  119.2 4.0 %collective-permute-done.24.refs_3_ = bf16[2,128,256]{2,1,0:T(8,128)(2,1)S(1)} collective-permute-done((bf16[2,128,256]{2,1,0:T(8,128)(2,1)S(1)}, bf16[2,128,256]{2,1,0:T(8,128)(2,1)S(1)}, u32[]{:S(2)}, u32[]{:S(2)}) %collective-permute-start.24) | collective-permute-done | bytes 131104 | tf_op jit(solution)/shard_map/ppermute | solution.py:41
  123.2 5.6 %collective-permute-start.33 = (bf16[512,256]{1,0:T(8,128)(2,1)S(1)}, bf16[512,256]{1,0:T(8,128)(2,1)S(1)}, u32[]{:S(2)}, u32[]{:S(2)}) collective-permute-start(bf16[512,256]{1,0:T(8,128)(2,1)S(1)} %pack.2), channel_id=1, source_target_pairs={{0,4},{4,0},{8,12},{12,8},{16,20},{20,16},{24,28},{28,24},{32,36},... | collective-permute-start | bytes 786440 | tf_op jit(solution)/shard_map/ppermute | solution.py:41
  128.8 1.4 collective-permute-start.34
  130.2 1.1 squares.1
  131.3 4.8 %all-to-all-start = ((f32[32,1,256]{2,1,0:T(1,128)}), f32[32,1,256]{2,1,0:T(1,128)S(1)}, u32[]{:S(2)}, u32[]{:S(2)}) async-start(f32[32,1,256]{2,1,0:T(1,128)} %squares.1), calls=%async_computation | async-start | bytes 65536 | tf_op jit(solution)/shard_map/all_to_all | solution.py:495
  137.5 0.9 copy-done.4
  138.5 1.3 place.1
  139.8 3.6 %all-to-all-done.sums_ref = f32[32,1,256]{2,1,0:T(1,128)S(1)} async-done(((f32[32,1,256]{2,1,0:T(1,128)}), f32[32,1,256]{2,1,0:T(1,128)S(1)}, u32[]{:S(2)}, u32[]{:S(2)}) %all-to-all-start) | async-done | bytes 32800 | tf_op jit(solution)/shard_map/all_to_all | solution.py:495
  143.4 1.4 finish.1
  (68 shorter events, 7.1 us)
Async XLA Ops:
  1.5 6.8 %collective-permute-start = (bf16[128,512]{1,0:T(8,128)(2,1)S(1)}, bf16[128,512]{1,0:T(8,128)(2,1)S(1)}, u32[]{:S(2)}, u32[]{:S(2)}) collective-permute-start(bf16[128,512]{1,0:T(8,128)(2,1)S(1)} %join.1.refs_4_), channel_id=1, source_target_pairs={{0,32},{4,36},{8,40},{12,44},{16,48},{20,52},{24,56},{28,60},{32,6... | collective-permute-start | bytes 393224 | tf_op jit(solution)/shard_map/ppermute | solution.py:41
  3.6 8.2 %collective-permute-start.1 = (bf16[128,512]{1,0:T(8,128)(2,1)S(1)}, bf16[128,512]{1,0:T(8,128)(2,1)S(1)}, u32[]{:S(2)}, u32[]{:S(2)}) collective-permute-start(bf16[128,512]{1,0:T(8,128)(2,1)S(1)} %join.1.refs_4_), channel_id=1, source_target_pairs={{0,24},{4,28},{8,32},{12,36},{16,40},{20,44},{24,48},{28,52},{32,5... | collective-permute-start | bytes 393224 | tf_op jit(solution)/shard_map/ppermute | solution.py:41
  6.4 9.9 %collective-permute-start.2 = (bf16[128,512]{1,0:T(8,128)(2,1)S(1)}, bf16[128,512]{1,0:T(8,128)(2,1)S(1)}, u32[]{:S(2)}, u32[]{:S(2)}) collective-permute-start(bf16[128,512]{1,0:T(8,128)(2,1)S(1)} %join.1.refs_4_), channel_id=1, source_target_pairs={{0,16},{4,20},{8,24},{12,28},{16,32},{20,36},{24,40},{28,44},{32,4... | collective-permute-start | bytes 393224 | tf_op jit(solution)/shard_map/ppermute | solution.py:41
  7.6 11.2 %collective-permute-start.3 = (bf16[128,512]{1,0:T(8,128)(2,1)S(1)}, bf16[128,512]{1,0:T(8,128)(2,1)S(1)}, u32[]{:S(2)}, u32[]{:S(2)}) collective-permute-start(bf16[128,512]{1,0:T(8,128)(2,1)S(1)} %join.1.refs_4_), channel_id=1, source_target_pairs={{0,8},{4,12},{8,16},{12,20},{16,24},{20,28},{24,32},{28,36},{32,40... | collective-permute-start | bytes 393224 | tf_op jit(solution)/shard_map/ppermute | solution.py:41
  19.0 7.4 %copy-start.2 = (bf16[128,2048]{1,0:T(8,128)(2,1)S(1)}, bf16[128,2048]{1,0:T(8,128)(2,1)}, u32[]{:S(2)}) copy-start(bf16[128,2048]{1,0:T(8,128)(2,1)} %q_ref.1) | copy-start | bytes 1572868
  19.0 7.5 %collective-permute-start.4 = (bf16[512,512]{1,0:T(8,128)(2,1)S(1)}, bf16[512,512]{1,0:T(8,128)(2,1)S(1)}, u32[]{:S(2)}, u32[]{:S(2)}) collective-permute-start(bf16[512,512]{1,0:T(8,128)(2,1)S(1)} %get-tuple-element.31), channel_id=1, source_target_pairs={{0,4},{4,0},{8,12},{12,8},{16,20},{20,16},{24,28},{28,24},{32,36},... | collective-permute-start | bytes 1572872 | tf_op jit(solution)/shard_map/ppermute | solution.py:41
  20.9 5.5 %copy-start.5 = (s32[4096]{0:T(1024)S(1)}, s32[4096]{0:T(1024)}, u32[]{:S(2)}) copy-start(s32[4096]{0:T(1024)} %param.11) | copy-start | bytes 49156
  22.2 14.7 %collective-permute-start.13 = (bf16[1024,256]{1,0:T(8,128)(2,1)S(1)}, bf16[1024,256]{1,0:T(8,128)(2,1)S(1)}, u32[]{:S(2)}, u32[]{:S(2)}) collective-permute-start(bf16[1024,256]{1,0:T(8,128)(2,1)S(1)} %get-tuple-element.57), channel_id=1, source_target_pairs={{0,8},{4,12},{8,16},{12,20},{16,24},{20,28},{24,0},{28,4},{32,40},... | collective-permute-start | bytes 1572872 | tf_op jit(solution)/shard_map/ppermute | solution.py:41
  22.3 25.9 %collective-permute-start.14 = (bf16[1024,256]{1,0:T(8,128)(2,1)S(1)}, bf16[1024,256]{1,0:T(8,128)(2,1)S(1)}, u32[]{:S(2)}, u32[]{:S(2)}) collective-permute-start(bf16[1024,256]{1,0:T(8,128)(2,1)S(1)} %get-tuple-element.56), channel_id=1, source_target_pairs={{0,8},{4,12},{8,16},{12,20},{16,24},{20,28},{24,0},{28,4},{32,40},... | collective-permute-start | bytes 1572872 | tf_op jit(solution)/shard_map/ppermute | solution.py:41
  22.4 26.7 %collective-permute-start.17 = (bf16[1024,256]{1,0:T(8,128)(2,1)S(1)}, bf16[1024,256]{1,0:T(8,128)(2,1)S(1)}, u32[]{:S(2)}, u32[]{:S(2)}) collective-permute-start(bf16[1024,256]{1,0:T(8,128)(2,1)S(1)} %get-tuple-element.57), channel_id=1, source_target_pairs={{0,24},{4,28},{8,0},{12,4},{16,8},{20,12},{24,16},{28,20},{32,56},... | collective-permute-start | bytes 1572872 | tf_op jit(solution)/shard_map/ppermute | solution.py:41
  25.0 25.3 %collective-permute-start.18 = (bf16[1024,256]{1,0:T(8,128)(2,1)S(1)}, bf16[1024,256]{1,0:T(8,128)(2,1)S(1)}, u32[]{:S(2)}, u32[]{:S(2)}) collective-permute-start(bf16[1024,256]{1,0:T(8,128)(2,1)S(1)} %get-tuple-element.56), channel_id=1, source_target_pairs={{0,24},{4,28},{8,0},{12,4},{16,8},{20,12},{24,16},{28,20},{32,56},... | collective-permute-start | bytes 1572872 | tf_op jit(solution)/shard_map/ppermute | solution.py:41
  26.5 30.4 %copy-start = (bf16[2048,256]{1,0:T(8,128)(2,1)S(1)}, bf16[2048,256]{1,0:T(8,128)(2,1)}, u32[]{:S(2)}) copy-start(bf16[2048,256]{1,0:T(8,128)(2,1)} %refs_4_.3) | copy-start | bytes 3145732
  26.5 53.8 %copy-start.1 = (bf16[2048,256]{1,0:T(8,128)(2,1)S(1)}, bf16[2048,256]{1,0:T(8,128)(2,1)}, u32[]{:S(2)}) copy-start(bf16[2048,256]{1,0:T(8,128)(2,1)} %residual_ref.3) | copy-start | bytes 3145732
  29.9 20.6 %collective-permute-start.5 = (bf16[64,2048]{1,0:T(8,128)(2,1)S(1)}, bf16[64,2048]{1,0:T(8,128)(2,1)S(1)}, u32[]{:S(2)}, u32[]{:S(2)}) collective-permute-start(bf16[64,2048]{1,0:T(8,128)(2,1)S(1)} %get-tuple-element.34.refs_0_), channel_id=1, source_target_pairs={{0,32},{4,36},{8,40},{12,44},{16,48},{20,52},{24,56},{28,60},{32,6... | collective-permute-start | bytes 786440 | tf_op jit(solution)/shard_map/ppermute | solution.py:41
  36.9 15.2 %collective-permute-start.6 = (bf16[64,2048]{1,0:T(8,128)(2,1)S(1)}, bf16[64,2048]{1,0:T(8,128)(2,1)S(1)}, u32[]{:S(2)}, u32[]{:S(2)}) collective-permute-start(bf16[64,2048]{1,0:T(8,128)(2,1)S(1)} %get-tuple-element.34.refs_0_), channel_id=1, source_target_pairs={{0,64},{4,68},{8,72},{12,76},{16,80},{20,84},{24,88},{28,92},{32,9... | collective-permute-start | bytes 786440 | tf_op jit(solution)/shard_map/ppermute | solution.py:41
  48.1 19.3 %collective-permute-start.15 = (bf16[1024,256]{1,0:T(8,128)(2,1)S(1)}, bf16[1024,256]{1,0:T(8,128)(2,1)S(1)}, u32[]{:S(2)}, u32[]{:S(2)}) collective-permute-start(bf16[1024,256]{1,0:T(8,128)(2,1)S(1)} %collective-permute-done.13.refs_6_.refs_4_), channel_id=1, source_target_pairs={{0,4},{4,0},{8,12},{12,8},{16,20},{20,16},{24,28},{28,24},{32,36},... | collective-permute-start | bytes 1572872 | tf_op jit(solution)/shard_map/ppermute | solution.py:41
  49.0 7.9 %collective-permute-start.7 = (bf16[64,2048]{1,0:T(8,128)(2,1)S(1)}, bf16[64,2048]{1,0:T(8,128)(2,1)S(1)}, u32[]{:S(2)}, u32[]{:S(2)}) collective-permute-start(bf16[64,2048]{1,0:T(8,128)(2,1)S(1)} %get-tuple-element.34.refs_0_), channel_id=1, source_target_pairs={{0,96},{4,100},{8,104},{12,108},{16,112},{20,116},{24,120},{28,124... | collective-permute-start | bytes 786440 | tf_op jit(solution)/shard_map/ppermute | solution.py:41
  50.3 14.4 %collective-permute-start.10 = (bf16[64,2048]{1,0:T(8,128)(2,1)S(1)}, bf16[64,2048]{1,0:T(8,128)(2,1)S(1)}, u32[]{:S(2)}, u32[]{:S(2)}) collective-permute-start(bf16[64,2048]{1,0:T(8,128)(2,1)S(1)} %get-tuple-element.37.refs_0_.refs_4_), channel_id=1, source_target_pairs={{0,32},{4,36},{8,40},{12,44},{16,48},{20,52},{24,56},{28,60},{32,6... | collective-permute-start | bytes 786440 | tf_op jit(solution)/shard_map/ppermute | solution.py:41
  50.5 14.2 %collective-permute-start.11 = (bf16[64,2048]{1,0:T(8,128)(2,1)S(1)}, bf16[64,2048]{1,0:T(8,128)(2,1)S(1)}, u32[]{:S(2)}, u32[]{:S(2)}) collective-permute-start(bf16[64,2048]{1,0:T(8,128)(2,1)S(1)} %get-tuple-element.37.refs_0_.refs_4_), channel_id=1, source_target_pairs={{0,64},{4,68},{8,72},{12,76},{16,80},{20,84},{24,88},{28,92},{32,9... | collective-permute-start | bytes 786440 | tf_op jit(solution)/shard_map/ppermute | solution.py:41
  52.0 17.1 %collective-permute-start.16 = (bf16[1024,256]{1,0:T(8,128)(2,1)S(1)}, bf16[1024,256]{1,0:T(8,128)(2,1)S(1)}, u32[]{:S(2)}, u32[]{:S(2)}) collective-permute-start(bf16[1024,256]{1,0:T(8,128)(2,1)S(1)} %collective-permute-done.14.refs_7_.refs_5_), channel_id=1, source_target_pairs={{0,4},{4,0},{8,12},{12,8},{16,20},{20,16},{24,28},{28,24},{32,36},... | collective-permute-start | bytes 1572872 | tf_op jit(solution)/shard_map/ppermute | solution.py:41
  56.9 32.4 %collective-permute-start.8 = (bf16[2048,256]{1,0:T(8,128)(2,1)S(1)}, bf16[2048,256]{1,0:T(8,128)(2,1)S(1)}, u32[]{:S(2)}, u32[]{:S(2)}) collective-permute-start(bf16[2048,256]{1,0:T(8,128)(2,1)S(1)} %copy-done), channel_id=1, source_target_pairs={{0,4},{4,0},{8,12},{12,8},{16,20},{20,16},{24,28},{28,24},{32,36},... | collective-permute-start | bytes 3145736 | tf_op jit(solution)/shard_map/ppermute | solution.py:41
  64.7 13.6 %collective-permute-start.27 = (bf16[1024,256]{1,0:T(8,128)(2,1)S(1)}, bf16[1024,256]{1,0:T(8,128)(2,1)S(1)}, u32[]{:S(2)}, u32[]{:S(2)}) collective-permute-start(bf16[1024,256]{1,0:T(8,128)(2,1)S(1)} %collective-permute-done.13.refs_6_.refs_4_), channel_id=1, source_target_pairs={{0,8},{4,12},{8,16},{12,20},{16,24},{20,28},{24,0},{28,4},{32,40},... | collective-permute-start | bytes 1572872 | tf_op jit(solution)/shard_map/ppermute | solution.py:41
  64.7 15.5 %collective-permute-start.28 = (bf16[1024,256]{1,0:T(8,128)(2,1)S(1)}, bf16[1024,256]{1,0:T(8,128)(2,1)S(1)}, u32[]{:S(2)}, u32[]{:S(2)}) collective-permute-start(bf16[1024,256]{1,0:T(8,128)(2,1)S(1)} %collective-permute-done.18.refs_11_.refs_9_), channel_id=1, source_target_pairs={{0,24},{4,28},{8,0},{12,4},{16,8},{20,12},{24,16},{28,20},{32,56},... | collective-permute-start | bytes 1572872 | tf_op jit(solution)/shard_map/ppermute | solution.py:41
  67.4 12.9 %collective-permute-start.19 = (bf16[1024,256]{1,0:T(8,128)(2,1)S(1)}, bf16[1024,256]{1,0:T(8,128)(2,1)S(1)}, u32[]{:S(2)}, u32[]{:S(2)}) collective-permute-start(bf16[1024,256]{1,0:T(8,128)(2,1)S(1)} %collective-permute-done.17.refs_10_.refs_8_), channel_id=1, source_target_pairs={{0,4},{4,0},{8,12},{12,8},{16,20},{20,16},{24,28},{28,24},{32,36},... | collective-permute-start | bytes 1572872 | tf_op jit(solution)/shard_map/ppermute | solution.py:41
  69.1 11.4 %collective-permute-start.20 = (bf16[1024,256]{1,0:T(8,128)(2,1)S(1)}, bf16[1024,256]{1,0:T(8,128)(2,1)S(1)}, u32[]{:S(2)}, u32[]{:S(2)}) collective-permute-start(bf16[1024,256]{1,0:T(8,128)(2,1)S(1)} %collective-permute-done.18.refs_11_.refs_9_), channel_id=1, source_target_pairs={{0,4},{4,0},{8,12},{12,8},{16,20},{20,16},{24,28},{28,24},{32,36},... | collective-permute-start | bytes 1572872 | tf_op jit(solution)/shard_map/ppermute | solution.py:41
  78.3 14.4 %collective-permute-start.29 = (bf16[1024,256]{1,0:T(8,128)(2,1)S(1)}, bf16[1024,256]{1,0:T(8,128)(2,1)S(1)}, u32[]{:S(2)}, u32[]{:S(2)}) collective-permute-start(bf16[1024,256]{1,0:T(8,128)(2,1)S(1)} %collective-permute-done.27.refs_8_), channel_id=1, source_target_pairs={{0,4},{4,0},{8,12},{12,8},{16,20},{20,16},{24,28},{28,24},{32,36},... | collective-permute-start | bytes 1572872 | tf_op jit(solution)/shard_map/ppermute | solution.py:41
  80.3 14.3 %collective-permute-start.30 = (bf16[1024,256]{1,0:T(8,128)(2,1)S(1)}, bf16[1024,256]{1,0:T(8,128)(2,1)S(1)}, u32[]{:S(2)}, u32[]{:S(2)}) collective-permute-start(bf16[1024,256]{1,0:T(8,128)(2,1)S(1)} %collective-permute-done.28.refs_9_), channel_id=1, source_target_pairs={{0,4},{4,0},{8,12},{12,8},{16,20},{20,16},{24,28},{28,24},{32,36},... | collective-permute-start | bytes 1572872 | tf_op jit(solution)/shard_map/ppermute | solution.py:41
  80.3 7.5 %collective-permute-start.12 = (bf16[64,2048]{1,0:T(8,128)(2,1)S(1)}, bf16[64,2048]{1,0:T(8,128)(2,1)S(1)}, u32[]{:S(2)}, u32[]{:S(2)}) collective-permute-start(bf16[64,2048]{1,0:T(8,128)(2,1)S(1)} %get-tuple-element.37.refs_0_.refs_4_), channel_id=1, source_target_pairs={{0,96},{4,100},{8,104},{12,108},{16,112},{20,116},{24,120},{28,124... | collective-permute-start | bytes 786440 | tf_op jit(solution)/shard_map/ppermute | solution.py:41
  80.5 15.6 %collective-permute-start.35 = (bf16[2,256,256]{2,1,0:T(8,128)(2,1)S(1)}, bf16[2,256,256]{2,1,0:T(8,128)(2,1)S(1)}, u32[]{:S(2)}, u32[]{:S(2)}) collective-permute-start(bf16[2,256,256]{2,1,0:T(8,128)(2,1)S(1)} %get-tuple-element.52), channel_id=1, source_target_pairs={{0,8},{4,12},{8,16},{12,20},{16,24},{20,28},{24,0},{28,4},{32,40},... | collective-permute-start | bytes 786440 | tf_op jit(solution)/shard_map/ppermute | solution.py:41
  87.8 9.8 %collective-permute-start.36 = (bf16[2,256,256]{2,1,0:T(8,128)(2,1)S(1)}, bf16[2,256,256]{2,1,0:T(8,128)(2,1)S(1)}, u32[]{:S(2)}, u32[]{:S(2)}) collective-permute-start(bf16[2,256,256]{2,1,0:T(8,128)(2,1)S(1)} %get-tuple-element.53), channel_id=1, source_target_pairs={{0,16},{4,20},{8,24},{12,28},{16,0},{20,4},{24,8},{28,12},{32,48},... | collective-permute-start | bytes 786440 | tf_op jit(solution)/shard_map/ppermute | solution.py:41
  89.3 13.3 %collective-permute-start.37 = (bf16[2,256,256]{2,1,0:T(8,128)(2,1)S(1)}, bf16[2,256,256]{2,1,0:T(8,128)(2,1)S(1)}, u32[]{:S(2)}, u32[]{:S(2)}) collective-permute-start(bf16[2,256,256]{2,1,0:T(8,128)(2,1)S(1)} %get-tuple-element.54), channel_id=1, source_target_pairs={{0,24},{4,28},{8,0},{12,4},{16,8},{20,12},{24,16},{28,20},{32,56},... | collective-permute-start | bytes 786440 | tf_op jit(solution)/shard_map/ppermute | solution.py:41
  92.7 23.7 %collective-permute-start.21 = (bf16[128,1536]{1,0:T(8,128)(2,1)S(1)}, bf16[128,1536]{1,0:T(8,128)(2,1)S(1)}, u32[]{:S(2)}, u32[]{:S(2)}) collective-permute-start(bf16[128,1536]{1,0:T(8,128)(2,1)S(1)} %get-tuple-element.39), channel_id=1, source_target_pairs={{0,128},{128,0},{1,129},{129,1},{2,130},{130,2},{3,131},{131,3},{4... | collective-permute-start | bytes 1179656 | tf_op jit(solution)/shard_map/ppermute | solution.py:474
  94.6 13.9 %collective-permute-start.22 = (bf16[128,1024]{1,0:T(8,128)(2,1)S(1)}, bf16[128,1024]{1,0:T(8,128)(2,1)S(1)}, u32[]{:S(2)}, u32[]{:S(2)}) collective-permute-start(bf16[128,1024]{1,0:T(8,128)(2,1)S(1)} %get-tuple-element.42), channel_id=1, source_target_pairs={{0,128},{128,0},{1,129},{129,1},{2,130},{130,2},{3,131},{131,3},{4... | collective-permute-start | bytes 786440 | tf_op jit(solution)/shard_map/ppermute | solution.py:474
  96.1 18.0 %collective-permute-start.31 = (bf16[256,512]{1,0:T(8,128)(2,1)S(1)}, bf16[256,512]{1,0:T(8,128)(2,1)S(1)}, u32[]{:S(2)}, u32[]{:S(2)}) collective-permute-start(bf16[256,512]{1,0:T(8,128)(2,1)S(1)} %get-tuple-element.48), channel_id=1, source_target_pairs={{0,128},{128,0},{1,129},{129,1},{2,130},{130,2},{3,131},{131,3},{4... | collective-permute-start | bytes 786440 | tf_op jit(solution)/shard_map/ppermute | solution.py:474
  102.7 27.5 %collective-permute-start.38 = (bf16[4,2,128,256]{3,2,1,0:T(8,128)(2,1)S(1)}, bf16[4,2,128,256]{3,2,1,0:T(8,128)(2,1)S(1)}, u32[]{:S(2)}, u32[]{:S(2)}) collective-permute-start(bf16[4,2,128,256]{3,2,1,0:T(8,128)(2,1)S(1)} %trade.1), channel_id=1, source_target_pairs={{0,4},{4,0},{8,12},{12,8},{16,20},{20,16},{24,28},{28,24},{32,36},... | collective-permute-start | bytes 1572872 | tf_op jit(solution)/shard_map/ppermute | solution.py:41
  105.2 11.7 %collective-permute-start.9 = (bf16[128,512]{1,0:T(8,128)(2,1)S(1)}, bf16[128,512]{1,0:T(8,128)(2,1)S(1)}, u32[]{:S(2)}, u32[]{:S(2)}) collective-permute-start(bf16[128,512]{1,0:T(8,128)(2,1)S(1)} %get-tuple-element.36), channel_id=1, source_target_pairs={{0,128},{128,0},{1,129},{129,1},{2,130},{130,2},{3,131},{131,3},{4... | collective-permute-start | bytes 393224 | tf_op jit(solution)/shard_map/ppermute | solution.py:474
  108.5 10.6 %collective-permute-start.23 = (bf16[2,128,256]{2,1,0:T(8,128)(2,1)S(1)}, bf16[2,128,256]{2,1,0:T(8,128)(2,1)S(1)}, u32[]{:S(2)}, u32[]{:S(2)}) collective-permute-start(bf16[2,128,256]{2,1,0:T(8,128)(2,1)S(1)} %get-tuple-element.43.refs_2_), channel_id=1, source_target_pairs={{0,24},{4,28},{8,0},{12,4},{16,8},{20,12},{24,16},{28,20},{32,56},... | collective-permute-start | bytes 393224 | tf_op jit(solution)/shard_map/ppermute | solution.py:41
  114.1 14.6 %collective-permute-start.32 = (bf16[2,256,256]{2,1,0:T(8,128)(2,1)S(1)}, bf16[2,256,256]{2,1,0:T(8,128)(2,1)S(1)}, u32[]{:S(2)}, u32[]{:S(2)}) collective-permute-start(bf16[2,256,256]{2,1,0:T(8,128)(2,1)S(1)} %combine.7.refs_6_), channel_id=1, source_target_pairs={{0,16},{4,20},{8,24},{12,28},{16,0},{20,4},{24,8},{28,12},{32,48},... | collective-permute-start | bytes 786440 | tf_op jit(solution)/shard_map/ppermute | solution.py:41
  116.3 6.9 %collective-permute-start.24 = (bf16[2,128,256]{2,1,0:T(8,128)(2,1)S(1)}, bf16[2,128,256]{2,1,0:T(8,128)(2,1)S(1)}, u32[]{:S(2)}, u32[]{:S(2)}) collective-permute-start(bf16[2,128,256]{2,1,0:T(8,128)(2,1)S(1)} %get-tuple-element.44.refs_4_), channel_id=1, source_target_pairs={{0,8},{4,12},{8,16},{12,20},{16,24},{20,28},{24,0},{28,4},{32,40},... | collective-permute-start | bytes 393224 | tf_op jit(solution)/shard_map/ppermute | solution.py:41
  116.9 11.9 %collective-permute-start.25 = (bf16[2,128,256]{2,1,0:T(8,128)(2,1)S(1)}, bf16[2,128,256]{2,1,0:T(8,128)(2,1)S(1)}, u32[]{:S(2)}, u32[]{:S(2)}) collective-permute-start(bf16[2,128,256]{2,1,0:T(8,128)(2,1)S(1)} %get-tuple-element.45.refs_3_), channel_id=1, source_target_pairs={{0,24},{4,28},{8,0},{12,4},{16,8},{20,12},{24,16},{28,20},{32,56},... | collective-permute-start | bytes 393224 | tf_op jit(solution)/shard_map/ppermute | solution.py:41
  119.2 9.6 %collective-permute-start.26 = (bf16[2,128,256]{2,1,0:T(8,128)(2,1)S(1)}, bf16[2,128,256]{2,1,0:T(8,128)(2,1)S(1)}, u32[]{:S(2)}, u32[]{:S(2)}) collective-permute-start(bf16[2,128,256]{2,1,0:T(8,128)(2,1)S(1)} %get-tuple-element.46.refs_5_), channel_id=1, source_target_pairs={{0,8},{4,12},{8,16},{12,20},{16,24},{20,28},{24,0},{28,4},{32,40},... | collective-permute-start | bytes 393224 | tf_op jit(solution)/shard_map/ppermute | solution.py:41
  123.2 12.9 %collective-permute-start.33 = (bf16[512,256]{1,0:T(8,128)(2,1)S(1)}, bf16[512,256]{1,0:T(8,128)(2,1)S(1)}, u32[]{:S(2)}, u32[]{:S(2)}) collective-permute-start(bf16[512,256]{1,0:T(8,128)(2,1)S(1)} %pack.2), channel_id=1, source_target_pairs={{0,4},{4,0},{8,12},{12,8},{16,20},{20,16},{24,28},{28,24},{32,36},... | collective-permute-start | bytes 786440 | tf_op jit(solution)/shard_map/ppermute | solution.py:41
  128.8 7.3 %collective-permute-start.34 = (bf16[512,256]{1,0:T(8,128)(2,1)S(1)}, bf16[512,256]{1,0:T(8,128)(2,1)S(1)}, u32[]{:S(2)}, u32[]{:S(2)}) collective-permute-start(bf16[512,256]{1,0:T(8,128)(2,1)S(1)} %pack.3), channel_id=1, source_target_pairs={{0,4},{4,0},{8,12},{12,8},{16,20},{20,16},{24,28},{28,24},{32,36},... | collective-permute-start | bytes 786440 | tf_op jit(solution)/shard_map/ppermute | solution.py:41
  130.2 6.6 %copy-start.7 = (s32[256]{0:T(256)S(1)}, s32[256]{0:T(256)}, u32[]{:S(2)}) copy-start(s32[256]{0:T(256)} %param.15) | copy-start | bytes 3076
  131.3 12.1 %all-to-all-start = ((f32[32,1,256]{2,1,0:T(1,128)}), f32[32,1,256]{2,1,0:T(1,128)S(1)}, u32[]{:S(2)}, u32[]{:S(2)}) async-start(f32[32,1,256]{2,1,0:T(1,128)} %squares.1), calls=%async_computation | async-start | bytes 65536 | tf_op jit(solution)/shard_map/all_to_all | solution.py:495
  136.1 0.7 copy-start.3
  136.8 0.7 copy-start.6
  137.5 0.9 copy-start.4
where the time goes:
time: 145 us
  waiting for transfers between devices  72.4 us (50%)
  starting transfers between devices  54 us (37%)
  Pallas kernels  13.8 us (10%)
  local copies, waits for them, and re-layouts  3.63 us (3%)
    ppermute x35, waiting for transfers between devices, send(): return lax.ppermute(value, 'sp', perm)  61.7 us
    ppermute x35, starting transfers between devices, send(): return lax.ppermute(value, 'sp', perm)  44 us
    ppermute x4, waiting for transfers between devices, across(): got = lax.ppermute(give, 'tp', [(0, 1), (1, 0)])  7.06 us
    pallas_call x4, Pallas kernels, project(): pl.pallas_call(functools.partial(project_kernel, sets, splits), out_shape...  5.29 us
    ppermute x4, starting transfers between devices, across(): got = lax.ppermute(give, 'tp', [(0, 1), (1, 0)])  5.21 us
    all_to_all x1, starting transfers between devices, inner(): sums = lax.all_to_all(squares, 'sp', 0, 0, tiled=True)  4.79 us
    all_to_all x1, waiting for transfers between devices, inner(): sums = lax.all_to_all(squares, 'sp', 0, 0, tiled=True)  3.62 us
    pallas_call x1, Pallas kernels, attend(): pl.pallas_call(attention_kernel, out_shape=tuple((pltpu.VMEM((size, width...  3.34 us
  transfers between devices with their start and end apart: 40, of which 15 were waited for; matrix products, arithmetic and copies ran while one was open for 1% of the time, Pallas kernels for 8%

commit v1 on v0

--- a/solution.py
+++ b/solution.py
@@ -15,7 +15,7 @@
 SIZES = (64, 64)
 LOWS = (0, 64)
 CHUNKS = len(SIZES)
-STACKED = 4
+STACKED = 8
 
 epsilon = 1e-05
 limit_value = 448.0
@@ -359,23 +359,19 @@
     )(*near(*lines))
 
 
-def squares_kernel(*refs):
-    pieces, lines, far_ref, out = refs[:7], refs[7:11], refs[11], refs[12]
+def squares_kernel(groups, final, *refs):
+    count = 2 * len([g for g in groups if g != 2]) + (1 if 2 in groups else 0)
+    pieces, lines, far_ref = refs[:count], refs[count : count + 4], refs[count + 4]
+    before, out = refs[count + 5 : -1], refs[-1]
     core = lax.rem(lax.axis_index("sp"), 2)
-    own, down, up, last = pieces[0:2], pieces[2:4], pieces[4:6], pieces[6]
     sums = []
     for i in range(2):
         halves = []
         for chunk in range(CHUNKS):
             rows, low = SIZES[chunk], LOWS[chunk]
-            total = jnp.zeros((rows, 256), jnp.float32)
-            sources = (
-                (own[chunk], i * rows),
-                (down[chunk], i * rows),
-                (last, 2 * low + i * rows),
-                (up[chunk], i * rows),
-            )
-            for r, (piece, at) in enumerate(sources):
+            total = before[0][i, low : low + rows, :] if before else jnp.zeros((rows, 256), jnp.float32)
+            for number, r in enumerate(groups):
+                piece, at = (pieces[0], 2 * low + i * rows) if r == 2 else (pieces[2 * number + chunk], i * rows)
                 start = pl.multiple_of(core * 128 + low, 16)
                 for k, res in enumerate(
                     (lines[r][i, pl.ds(start, rows), :], far_ref[r, i, low : low + rows, :])
@@ -384,21 +380,27 @@
                     wide = added.astype(jnp.bfloat16).astype(jnp.float32)
                     total = total + wide * wide
             halves.append(total)
-        block = jnp.sum(jnp.concatenate(halves, axis=0), axis=1, keepdims=True)
+        block = jnp.concatenate(halves, axis=0)
+        if not final:
+            out[i] = block
+            continue
+        block = jnp.sum(block, axis=1, keepdims=True)
         sums.append(jnp.transpose(jnp.broadcast_to(block, (128, 128)))[:1])
-    line = jnp.concatenate(sums, axis=1)
-    out[...] = jnp.broadcast_to(line[None], out.shape)
-
-
-def squares_of(pieces, lines, far):
-    return pl.pallas_call(
-        squares_kernel,
-        out_shape=pltpu.VMEM((32, 1, 256), jnp.float32),
-        in_specs=[VM] * 12,
+    if final:
+        line = jnp.concatenate(sums, axis=1)
+        out[...] = jnp.broadcast_to(line[None], out.shape)
+
+
+def squares_of(groups, pieces, lines, far, before=()):
+    final = len(before) > 0
+    return pl.pallas_call(
+        functools.partial(squares_kernel, groups, final),
+        out_shape=pltpu.VMEM((32, 1, 256) if final else (2, 128, 256), jnp.float32),
+        in_specs=[VM] * (len(pieces) + 5 + len(before)),
         out_specs=VM,
         compiler_params=limit(6),
         name="squares",
-    )(*near(*pieces, *lines, far))
+    )(*near(*pieces, *lines, far, *before))
 
 
 def finish_kernel(hidden_ref, sums_ref, table_ref, quantized_out):
@@ -491,7 +493,8 @@
         up.append(send(pieces[2], y_shift(1)))
     (piece,) = across(lines[0] + lines[1], far_weights)
     last = send(piece, y_shift(2))
-    squares = squares_of([made[c][g] for g in range(3) for c in range(2)] + [piece], res, res_far)
+    partial = squares_of((0, 1, 3), [made[c][g] for g in range(3) for c in range(2)], res, res_far)
+    squares = squares_of((2,), [piece], res, res_far, (partial,))
     sums = lax.all_to_all(squares, "sp", 0, 0, tiled=True)
     batches = [
         [(0, (0,), own[0]), (0, (1,), own[1]), (1, (0,), down[0]), (3, (0,), up[0])],

time: 145 us -> 145 us (level)
  no operation moved by 1% of the time
where the time goes in v1:
time: 145 us
  waiting for transfers between devices  72.3 us (50%)
  starting transfers between devices  54 us (37%)
  Pallas kernels  13.7 us (9%)
  local copies, waits for them, and re-layouts  3.63 us (3%)
    ppermute x35, waiting for transfers between devices, send(): return lax.ppermute(value, 'sp', perm)  62.1 us
    ppermute x35, starting transfers between devices, send(): return lax.ppermute(value, 'sp', perm)  44.2 us
    ppermute x4, waiting for transfers between devices, across(): got = lax.ppermute(give, 'tp', [(0, 1), (1, 0)])  6.62 us
    pallas_call x4, Pallas kernels, project(): pl.pallas_call(functools.partial(project_kernel, sets, splits), out_shape...  5.29 us
    ppermute x4, starting transfers between devices, across(): got = lax.ppermute(give, 'tp', [(0, 1), (1, 0)])  4.99 us
    all_to_all x1, starting transfers between devices, inner(): sums = lax.all_to_all(squares, 'sp', 0, 0, tiled=True)  4.79 us
    all_to_all x1, waiting for transfers between devices, inner(): sums = lax.all_to_all(squares, 'sp', 0, 0, tiled=True)  3.62 us
    pallas_call x1, Pallas kernels, attend(): pl.pallas_call(attention_kernel, out_shape=tuple((pltpu.VMEM((size, width...  3.19 us
  transfers between devices with their start and end apart: 40, of which 15 were waited for; matrix products, arithmetic and copies ran while one was open for 1% of the time, Pallas kernels for 8%

profile of v1, /device:TPU:1, one launch (start us, length us, event | category | flops | bytes accessed | tf_op | source)
XLA Modules:
  0.0 144.6 jit_solution(8460112753869347286)
XLA Ops:
  0.6 0.9 join.1.refs_4_
  1.5 2.1 %collective-permute-start = (bf16[128,512]{1,0:T(8,128)(2,1)S(1)}, bf16[128,512]{1,0:T(8,128)(2,1)S(1)}, u32[]{:S(2)}, u32[]{:S(2)}) collective-permute-start(bf16[128,512]{1,0:T(8,128)(2,1)S(1)} %join.1.refs_4_), channel_id=1, source_target_pairs={{0,32},{4,36},{8,40},{12,44},{16,48},{20,52},{24,56},{28,60},{32,6... | collective-permute-start | bytes 393224 | tf_op jit(solution)/shard_map/ppermute | solution.py:41
  3.6 2.7 %collective-permute-start.1 = (bf16[128,512]{1,0:T(8,128)(2,1)S(1)}, bf16[128,512]{1,0:T(8,128)(2,1)S(1)}, u32[]{:S(2)}, u32[]{:S(2)}) collective-permute-start(bf16[128,512]{1,0:T(8,128)(2,1)S(1)} %join.1.refs_4_), channel_id=1, source_target_pairs={{0,24},{4,28},{8,32},{12,36},{16,40},{20,44},{24,48},{28,52},{32,5... | collective-permute-start | bytes 393224 | tf_op jit(solution)/shard_map/ppermute | solution.py:41
  6.4 1.3 collective-permute-start.2
  8.3 3.5 %collective-permute-done.1.refs_1_ = bf16[128,512]{1,0:T(8,128)(2,1)S(1)} collective-permute-done((bf16[128,512]{1,0:T(8,128)(2,1)S(1)}, bf16[128,512]{1,0:T(8,128)(2,1)S(1)}, u32[]{:S(2)}, u32[]{:S(2)}) %collective-permute-start.1) | collective-permute-done | bytes 131104 | tf_op jit(solution)/shard_map/ppermute | solution.py:41
  11.8 4.4 %collective-permute-done.2.refs_2_ = bf16[128,512]{1,0:T(8,128)(2,1)S(1)} collective-permute-done((bf16[128,512]{1,0:T(8,128)(2,1)S(1)}, bf16[128,512]{1,0:T(8,128)(2,1)S(1)}, u32[]{:S(2)}, u32[]{:S(2)}) %collective-permute-start.2) | collective-permute-done | bytes 131104 | tf_op jit(solution)/shard_map/ppermute | solution.py:41
  16.3 2.6 %collective-permute-done.3.refs_3_ = bf16[128,512]{1,0:T(8,128)(2,1)S(1)} collective-permute-done((bf16[128,512]{1,0:T(8,128)(2,1)S(1)}, bf16[128,512]{1,0:T(8,128)(2,1)S(1)}, u32[]{:S(2)}, u32[]{:S(2)}) %collective-permute-start.3) | collective-permute-done | bytes 131104 | tf_op jit(solution)/shard_map/ppermute | solution.py:41
  19.0 1.9 %collective-permute-start.4 = (bf16[512,512]{1,0:T(8,128)(2,1)S(1)}, bf16[512,512]{1,0:T(8,128)(2,1)S(1)}, u32[]{:S(2)}, u32[]{:S(2)}) collective-permute-start(bf16[512,512]{1,0:T(8,128)(2,1)S(1)} %get-tuple-element.31), channel_id=1, source_target_pairs={{0,4},{4,0},{8,12},{12,8},{16,20},{20,16},{24,28},{28,24},{32,36},... | collective-permute-start | bytes 1572872 | tf_op jit(solution)/shard_map/ppermute | solution.py:41
  20.9 1.3 fusion
  22.4 2.7 %collective-permute-start.17 = (bf16[1024,256]{1,0:T(8,128)(2,1)S(1)}, bf16[1024,256]{1,0:T(8,128)(2,1)S(1)}, u32[]{:S(2)}, u32[]{:S(2)}) collective-permute-start(bf16[1024,256]{1,0:T(8,128)(2,1)S(1)} %get-tuple-element.57), channel_id=1, source_target_pairs={{0,24},{4,28},{8,0},{12,4},{16,8},{20,12},{24,16},{28,20},{32,56},... | collective-permute-start | bytes 1572872 | tf_op jit(solution)/shard_map/ppermute | solution.py:41
  25.0 1.4 collective-permute-start.18
  26.6 3.2 %attend.1 = (bf16[64,2048]{1,0:T(8,128)(2,1)S(1)}, bf16[64,2048]{1,0:T(8,128)(2,1)S(1)}) custom-call(bf16[128,2048]{1,0:T(8,128)(2,1)S(1)} %get-tuple-element.29.q_ref, bf16[640,512]{1,0:T(8,128)(2,1)S(1)} %get-tuple-element.30.a_ref, bf16[512,512]{1,0:T(8,128)(2,1)S(1)} %collective-permute-done.4.b_ref, f32[128,640]{1,0:T(8,128)S(1)} %get-tuple-element.32.bias_a, ...), custom_call_target="tpu_custom_call" | custom-call | flops 1811939328 | bytes 3145728 | tf_op jit(solution)/shard_map/attend/pallas_call | solution.py:178
  29.8 7.0 %collective-permute-done.13.refs_6_.refs_4_ = bf16[1024,256]{1,0:T(8,128)(2,1)S(1)} collective-permute-done((bf16[1024,256]{1,0:T(8,128)(2,1)S(1)}, bf16[1024,256]{1,0:T(8,128)(2,1)S(1)}, u32[]{:S(2)}, u32[]{:S(2)}) %collective-permute-start.13) | collective-permute-done | bytes 524320 | tf_op jit(solution)/shard_map/ppermute | solution.py:41
  36.9 1.5 %collective-permute-start.6 = (bf16[64,2048]{1,0:T(8,128)(2,1)S(1)}, bf16[64,2048]{1,0:T(8,128)(2,1)S(1)}, u32[]{:S(2)}, u32[]{:S(2)}) collective-permute-start(bf16[64,2048]{1,0:T(8,128)(2,1)S(1)} %get-tuple-element.34.refs_0_), channel_id=1, source_target_pairs={{0,64},{4,68},{8,72},{12,76},{16,80},{20,84},{24,88},{28,92},{32,9... | collective-permute-start | bytes 786440 | tf_op jit(solution)/shard_map/ppermute | solution.py:41
  38.4 9.7 %collective-permute-done.14.refs_7_.refs_5_ = bf16[1024,256]{1,0:T(8,128)(2,1)S(1)} collective-permute-done((bf16[1024,256]{1,0:T(8,128)(2,1)S(1)}, bf16[1024,256]{1,0:T(8,128)(2,1)S(1)}, u32[]{:S(2)}, u32[]{:S(2)}) %collective-permute-start.14) | collective-permute-done | bytes 524320 | tf_op jit(solution)/shard_map/ppermute | solution.py:41
  48.1 0.9 collective-permute-start.15
  49.0 1.3 collective-permute-start.7
  50.5 1.5 %collective-permute-start.11 = (bf16[64,2048]{1,0:T(8,128)(2,1)S(1)}, bf16[64,2048]{1,0:T(8,128)(2,1)S(1)}, u32[]{:S(2)}, u32[]{:S(2)}) collective-permute-start(bf16[64,2048]{1,0:T(8,128)(2,1)S(1)} %get-tuple-element.37.refs_0_.refs_4_), channel_id=1, source_target_pairs={{0,64},{4,68},{8,72},{12,76},{16,80},{20,84},{24,88},{28,92},{32,9... | collective-permute-start | bytes 786440 | tf_op jit(solution)/shard_map/ppermute | solution.py:41
  52.9 4.0 %collective-permute-done.7.refs_3_ = bf16[64,2048]{1,0:T(8,128)(2,1)S(1)} collective-permute-done((bf16[64,2048]{1,0:T(8,128)(2,1)S(1)}, bf16[64,2048]{1,0:T(8,128)(2,1)S(1)}, u32[]{:S(2)}, u32[]{:S(2)}) %collective-permute-start.7) | collective-permute-done | bytes 262176 | tf_op jit(solution)/shard_map/ppermute | solution.py:41
  56.9 1.3 collective-permute-start.8
  58.2 6.5 %collective-permute-done.10.refs_1_.refs_5_ = bf16[64,2048]{1,0:T(8,128)(2,1)S(1)} collective-permute-done((bf16[64,2048]{1,0:T(8,128)(2,1)S(1)}, bf16[64,2048]{1,0:T(8,128)(2,1)S(1)}, u32[]{:S(2)}, u32[]{:S(2)}) %collective-permute-start.10) | collective-permute-done | bytes 262176 | tf_op jit(solution)/shard_map/ppermute | solution.py:41
  64.7 2.7 %collective-permute-start.28 = (bf16[1024,256]{1,0:T(8,128)(2,1)S(1)}, bf16[1024,256]{1,0:T(8,128)(2,1)S(1)}, u32[]{:S(2)}, u32[]{:S(2)}) collective-permute-start(bf16[1024,256]{1,0:T(8,128)(2,1)S(1)} %collective-permute-done.18.refs_11_.refs_9_), channel_id=1, source_target_pairs={{0,24},{4,28},{8,0},{12,4},{16,8},{20,12},{24,16},{28,20},{32,56},... | collective-permute-start | bytes 1572872 | tf_op jit(solution)/shard_map/ppermute | solution.py:41
  67.4 1.7 %collective-permute-start.19 = (bf16[1024,256]{1,0:T(8,128)(2,1)S(1)}, bf16[1024,256]{1,0:T(8,128)(2,1)S(1)}, u32[]{:S(2)}, u32[]{:S(2)}) collective-permute-start(bf16[1024,256]{1,0:T(8,128)(2,1)S(1)} %collective-permute-done.17.refs_10_.refs_8_), channel_id=1, source_target_pairs={{0,4},{4,0},{8,12},{12,8},{16,20},{20,16},{24,28},{28,24},{32,36},... | collective-permute-start | bytes 1572872 | tf_op jit(solution)/shard_map/ppermute | solution.py:41
  69.2 9.1 %collective-permute-done.27.refs_8_ = bf16[1024,256]{1,0:T(8,128)(2,1)S(1)} collective-permute-done((bf16[1024,256]{1,0:T(8,128)(2,1)S(1)}, bf16[1024,256]{1,0:T(8,128)(2,1)S(1)}, u32[]{:S(2)}, u32[]{:S(2)}) %collective-permute-start.27) | collective-permute-done | bytes 524320 | tf_op jit(solution)/shard_map/ppermute | solution.py:41
  78.3 2.0 %collective-permute-start.29 = (bf16[1024,256]{1,0:T(8,128)(2,1)S(1)}, bf16[1024,256]{1,0:T(8,128)(2,1)S(1)}, u32[]{:S(2)}, u32[]{:S(2)}) collective-permute-start(bf16[1024,256]{1,0:T(8,128)(2,1)S(1)} %collective-permute-done.27.refs_8_), channel_id=1, source_target_pairs={{0,4},{4,0},{8,12},{12,8},{16,20},{20,16},{24,28},{28,24},{32,36},... | collective-permute-start | bytes 1572872 | tf_op jit(solution)/shard_map/ppermute | solution.py:41
  80.6 1.3 project.6
  81.9 5.9 %collective-permute-done.12.refs_3_.refs_7_ = bf16[64,2048]{1,0:T(8,128)(2,1)S(1)} collective-permute-done((bf16[64,2048]{1,0:T(8,128)(2,1)S(1)}, bf16[64,2048]{1,0:T(8,128)(2,1)S(1)}, u32[]{:S(2)}, u32[]{:S(2)}) %collective-permute-start.12) | collective-permute-done | bytes 262176 | tf_op jit(solution)/shard_map/ppermute | solution.py:41
  87.8 1.5 %collective-permute-start.36 = (bf16[2,256,256]{2,1,0:T(8,128)(2,1)S(1)}, bf16[2,256,256]{2,1,0:T(8,128)(2,1)S(1)}, u32[]{:S(2)}, u32[]{:S(2)}) collective-permute-start(bf16[2,256,256]{2,1,0:T(8,128)(2,1)S(1)} %get-tuple-element.53), channel_id=1, source_target_pairs={{0,16},{4,20},{8,24},{12,28},{16,0},{20,4},{24,8},{28,12},{32,48},... | collective-permute-start | bytes 786440 | tf_op jit(solution)/shard_map/ppermute | solution.py:41
  89.3 1.5 %collective-permute-start.37 = (bf16[2,256,256]{2,1,0:T(8,128)(2,1)S(1)}, bf16[2,256,256]{2,1,0:T(8,128)(2,1)S(1)}, u32[]{:S(2)}, u32[]{:S(2)}) collective-permute-start(bf16[2,256,256]{2,1,0:T(8,128)(2,1)S(1)} %get-tuple-element.54), channel_id=1, source_target_pairs={{0,24},{4,28},{8,0},{12,4},{16,8},{20,12},{24,16},{28,20},{32,56},... | collective-permute-start | bytes 786440 | tf_op jit(solution)/shard_map/ppermute | solution.py:41
  90.8 1.8 %project.5 = (bf16[128,1536]{1,0:T(8,128)(2,1)S(1)}, f32[128,1536]{1,0:T(8,128)S(1)}) custom-call(bf16[64,2048]{1,0:T(8,128)(2,1)S(1)} %get-tuple-element.37.refs_0_.refs_4_, bf16[64,2048]{1,0:T(8,128)(2,1)S(1)} %collective-permute-done.10.refs_1_.refs_5_, bf16[64,2048]{1,0:T(8,128)(2,1)S(1)} %collective-permute-done.11.refs_2_.refs_6_, ...), custom_call_target="tpu_custom_call" | custom-call | flops 1610612736 | bytes 8388608 | tf_op jit(solution)/shard_map/project/pallas_call | solution.py:223
  92.7 1.7 %collective-permute-start.21 = (bf16[128,1536]{1,0:T(8,128)(2,1)S(1)}, bf16[128,1536]{1,0:T(8,128)(2,1)S(1)}, u32[]{:S(2)}, u32[]{:S(2)}) collective-permute-start(bf16[128,1536]{1,0:T(8,128)(2,1)S(1)} %get-tuple-element.39), channel_id=1, source_target_pairs={{0,128},{128,0},{1,129},{129,1},{2,130},{130,2},{3,131},{131,3},{4... | collective-permute-start | bytes 1179656 | tf_op jit(solution)/shard_map/ppermute | solution.py:476
  94.7 1.4 project.7
  96.1 1.2 collective-permute-start.31
  97.4 5.3 %collective-permute-done.37.refs_3_.refs_9_.refs_4_ = bf16[2,256,256]{2,1,0:T(8,128)(2,1)S(1)} collective-permute-done((bf16[2,256,256]{2,1,0:T(8,128)(2,1)S(1)}, bf16[2,256,256]{2,1,0:T(8,128)(2,1)S(1)}, u32[]{:S(2)}, u32[]{:S(2)}) %collective-permute-start.37) | collective-permute-done | bytes 262176 | tf_op jit(solution)/shard_map/ppermute | solution.py:41
  102.7 1.8 %collective-permute-start.38 = (bf16[4,2,128,256]{3,2,1,0:T(8,128)(2,1)S(1)}, bf16[4,2,128,256]{3,2,1,0:T(8,128)(2,1)S(1)}, u32[]{:S(2)}, u32[]{:S(2)}) collective-permute-start(bf16[4,2,128,256]{3,2,1,0:T(8,128)(2,1)S(1)} %trade.1), channel_id=1, source_target_pairs={{0,4},{4,0},{8,12},{12,8},{16,20},{20,16},{24,28},{28,24},{32,36},... | collective-permute-start | bytes 1572872 | tf_op jit(solution)/shard_map/ppermute | solution.py:41
  105.2 1.7 %collective-permute-start.9 = (bf16[128,512]{1,0:T(8,128)(2,1)S(1)}, bf16[128,512]{1,0:T(8,128)(2,1)S(1)}, u32[]{:S(2)}, u32[]{:S(2)}) collective-permute-start(bf16[128,512]{1,0:T(8,128)(2,1)S(1)} %get-tuple-element.36), channel_id=1, source_target_pairs={{0,128},{128,0},{1,129},{129,1},{2,130},{130,2},{3,131},{131,3},{4... | collective-permute-start | bytes 393224 | tf_op jit(solution)/shard_map/ppermute | solution.py:476
  106.9 1.3 collective-permute-done.22.got_ref
  109.1 4.8 %collective-permute-done.31.got_ref = bf16[256,512]{1,0:T(8,128)(2,1)S(1)} collective-permute-done((bf16[256,512]{1,0:T(8,128)(2,1)S(1)}, bf16[256,512]{1,0:T(8,128)(2,1)S(1)}, u32[]{:S(2)}, u32[]{:S(2)}) %collective-permute-start.31) | collective-permute-done | bytes 262176 | tf_op jit(solution)/shard_map/ppermute | solution.py:476
  113.9 2.2 %collective-permute-start.32 = (bf16[2,256,256]{2,1,0:T(8,128)(2,1)S(1)}, bf16[2,256,256]{2,1,0:T(8,128)(2,1)S(1)}, u32[]{:S(2)}, u32[]{:S(2)}) collective-permute-start(bf16[2,256,256]{2,1,0:T(8,128)(2,1)S(1)} %combine.7.refs_0_), channel_id=1, source_target_pairs={{0,16},{4,20},{8,24},{12,28},{16,0},{20,4},{24,8},{28,12},{32,48},... | collective-permute-start | bytes 786440 | tf_op jit(solution)/shard_map/ppermute | solution.py:41
  116.7 2.2 %collective-permute-start.25 = (bf16[2,128,256]{2,1,0:T(8,128)(2,1)S(1)}, bf16[2,128,256]{2,1,0:T(8,128)(2,1)S(1)}, u32[]{:S(2)}, u32[]{:S(2)}) collective-permute-start(bf16[2,128,256]{2,1,0:T(8,128)(2,1)S(1)} %get-tuple-element.45.refs_3_), channel_id=1, source_target_pairs={{0,24},{4,28},{8,0},{12,4},{16,8},{20,12},{24,16},{28,20},{32,56},... | collective-permute-start | bytes 393224 | tf_op jit(solution)/shard_map/ppermute | solution.py:41
  119.0 4.0 %collective-permute-done.24.refs_3_ = bf16[2,128,256]{2,1,0:T(8,128)(2,1)S(1)} collective-permute-done((bf16[2,128,256]{2,1,0:T(8,128)(2,1)S(1)}, bf16[2,128,256]{2,1,0:T(8,128)(2,1)S(1)}, u32[]{:S(2)}, u32[]{:S(2)}) %collective-permute-start.24) | collective-permute-done | bytes 131104 | tf_op jit(solution)/shard_map/ppermute | solution.py:41
  123.0 5.6 %collective-permute-start.33 = (bf16[512,256]{1,0:T(8,128)(2,1)S(1)}, bf16[512,256]{1,0:T(8,128)(2,1)S(1)}, u32[]{:S(2)}, u32[]{:S(2)}) collective-permute-start(bf16[512,256]{1,0:T(8,128)(2,1)S(1)} %pack.2), channel_id=1, source_target_pairs={{0,4},{4,0},{8,12},{12,8},{16,20},{20,16},{24,28},{28,24},{32,36},... | collective-permute-start | bytes 786440 | tf_op jit(solution)/shard_map/ppermute | solution.py:41
  128.6 1.4 collective-permute-start.34
  131.1 4.8 %all-to-all-start = ((f32[32,1,256]{2,1,0:T(1,128)}), f32[32,1,256]{2,1,0:T(1,128)S(1)}, u32[]{:S(2)}, u32[]{:S(2)}) async-start(f32[32,1,256]{2,1,0:T(1,128)} %squares.3), calls=%async_computation | async-start | bytes 65536 | tf_op jit(solution)/shard_map/all_to_all | solution.py:498
  137.3 0.9 copy-done.4
  138.3 1.3 place.1
  139.6 3.6 %all-to-all-done.sums_ref = f32[32,1,256]{2,1,0:T(1,128)S(1)} async-done(((f32[32,1,256]{2,1,0:T(1,128)}), f32[32,1,256]{2,1,0:T(1,128)S(1)}, u32[]{:S(2)}, u32[]{:S(2)}) %all-to-all-start) | async-done | bytes 32800 | tf_op jit(solution)/shard_map/all_to_all | solution.py:498
  143.2 1.4 finish.1
  (69 shorter events, 7.8 us)
Async XLA Ops:
  1.5 6.8 %collective-permute-start = (bf16[128,512]{1,0:T(8,128)(2,1)S(1)}, bf16[128,512]{1,0:T(8,128)(2,1)S(1)}, u32[]{:S(2)}, u32[]{:S(2)}) collective-permute-start(bf16[128,512]{1,0:T(8,128)(2,1)S(1)} %join.1.refs_4_), channel_id=1, source_target_pairs={{0,32},{4,36},{8,40},{12,44},{16,48},{20,52},{24,56},{28,60},{32,6... | collective-permute-start | bytes 393224 | tf_op jit(solution)/shard_map/ppermute | solution.py:41
  3.6 8.2 %collective-permute-start.1 = (bf16[128,512]{1,0:T(8,128)(2,1)S(1)}, bf16[128,512]{1,0:T(8,128)(2,1)S(1)}, u32[]{:S(2)}, u32[]{:S(2)}) collective-permute-start(bf16[128,512]{1,0:T(8,128)(2,1)S(1)} %join.1.refs_4_), channel_id=1, source_target_pairs={{0,24},{4,28},{8,32},{12,36},{16,40},{20,44},{24,48},{28,52},{32,5... | collective-permute-start | bytes 393224 | tf_op jit(solution)/shard_map/ppermute | solution.py:41
  6.4 9.9 %collective-permute-start.2 = (bf16[128,512]{1,0:T(8,128)(2,1)S(1)}, bf16[128,512]{1,0:T(8,128)(2,1)S(1)}, u32[]{:S(2)}, u32[]{:S(2)}) collective-permute-start(bf16[128,512]{1,0:T(8,128)(2,1)S(1)} %join.1.refs_4_), channel_id=1, source_target_pairs={{0,16},{4,20},{8,24},{12,28},{16,32},{20,36},{24,40},{28,44},{32,4... | collective-permute-start | bytes 393224 | tf_op jit(solution)/shard_map/ppermute | solution.py:41
  7.6 11.2 %collective-permute-start.3 = (bf16[128,512]{1,0:T(8,128)(2,1)S(1)}, bf16[128,512]{1,0:T(8,128)(2,1)S(1)}, u32[]{:S(2)}, u32[]{:S(2)}) collective-permute-start(bf16[128,512]{1,0:T(8,128)(2,1)S(1)} %join.1.refs_4_), channel_id=1, source_target_pairs={{0,8},{4,12},{8,16},{12,20},{16,24},{20,28},{24,32},{28,36},{32,40... | collective-permute-start | bytes 393224 | tf_op jit(solution)/shard_map/ppermute | solution.py:41
  19.0 7.4 %copy-start.2 = (bf16[128,2048]{1,0:T(8,128)(2,1)S(1)}, bf16[128,2048]{1,0:T(8,128)(2,1)}, u32[]{:S(2)}) copy-start(bf16[128,2048]{1,0:T(8,128)(2,1)} %q_ref.1) | copy-start | bytes 1572868
  19.0 7.5 %collective-permute-start.4 = (bf16[512,512]{1,0:T(8,128)(2,1)S(1)}, bf16[512,512]{1,0:T(8,128)(2,1)S(1)}, u32[]{:S(2)}, u32[]{:S(2)}) collective-permute-start(bf16[512,512]{1,0:T(8,128)(2,1)S(1)} %get-tuple-element.31), channel_id=1, source_target_pairs={{0,4},{4,0},{8,12},{12,8},{16,20},{20,16},{24,28},{28,24},{32,36},... | collective-permute-start | bytes 1572872 | tf_op jit(solution)/shard_map/ppermute | solution.py:41
  20.9 5.5 %copy-start.5 = (s32[4096]{0:T(1024)S(1)}, s32[4096]{0:T(1024)}, u32[]{:S(2)}) copy-start(s32[4096]{0:T(1024)} %param.11) | copy-start | bytes 49156
  22.2 14.7 %collective-permute-start.13 = (bf16[1024,256]{1,0:T(8,128)(2,1)S(1)}, bf16[1024,256]{1,0:T(8,128)(2,1)S(1)}, u32[]{:S(2)}, u32[]{:S(2)}) collective-permute-start(bf16[1024,256]{1,0:T(8,128)(2,1)S(1)} %get-tuple-element.57), channel_id=1, source_target_pairs={{0,8},{4,12},{8,16},{12,20},{16,24},{20,28},{24,0},{28,4},{32,40},... | collective-permute-start | bytes 1572872 | tf_op jit(solution)/shard_map/ppermute | solution.py:41
  22.3 25.9 %collective-permute-start.14 = (bf16[1024,256]{1,0:T(8,128)(2,1)S(1)}, bf16[1024,256]{1,0:T(8,128)(2,1)S(1)}, u32[]{:S(2)}, u32[]{:S(2)}) collective-permute-start(bf16[1024,256]{1,0:T(8,128)(2,1)S(1)} %get-tuple-element.56), channel_id=1, source_target_pairs={{0,8},{4,12},{8,16},{12,20},{16,24},{20,28},{24,0},{28,4},{32,40},... | collective-permute-start | bytes 1572872 | tf_op jit(solution)/shard_map/ppermute | solution.py:41
  22.4 26.7 %collective-permute-start.17 = (bf16[1024,256]{1,0:T(8,128)(2,1)S(1)}, bf16[1024,256]{1,0:T(8,128)(2,1)S(1)}, u32[]{:S(2)}, u32[]{:S(2)}) collective-permute-start(bf16[1024,256]{1,0:T(8,128)(2,1)S(1)} %get-tuple-element.57), channel_id=1, source_target_pairs={{0,24},{4,28},{8,0},{12,4},{16,8},{20,12},{24,16},{28,20},{32,56},... | collective-permute-start | bytes 1572872 | tf_op jit(solution)/shard_map/ppermute | solution.py:41
  25.0 25.3 %collective-permute-start.18 = (bf16[1024,256]{1,0:T(8,128)(2,1)S(1)}, bf16[1024,256]{1,0:T(8,128)(2,1)S(1)}, u32[]{:S(2)}, u32[]{:S(2)}) collective-permute-start(bf16[1024,256]{1,0:T(8,128)(2,1)S(1)} %get-tuple-element.56), channel_id=1, source_target_pairs={{0,24},{4,28},{8,0},{12,4},{16,8},{20,12},{24,16},{28,20},{32,56},... | collective-permute-start | bytes 1572872 | tf_op jit(solution)/shard_map/ppermute | solution.py:41
  26.5 30.4 %copy-start = (bf16[2048,256]{1,0:T(8,128)(2,1)S(1)}, bf16[2048,256]{1,0:T(8,128)(2,1)}, u32[]{:S(2)}) copy-start(bf16[2048,256]{1,0:T(8,128)(2,1)} %refs_4_.3) | copy-start | bytes 3145732
  26.5 53.8 %copy-start.1 = (bf16[2048,256]{1,0:T(8,128)(2,1)S(1)}, bf16[2048,256]{1,0:T(8,128)(2,1)}, u32[]{:S(2)}) copy-start(bf16[2048,256]{1,0:T(8,128)(2,1)} %residual_ref.3) | copy-start | bytes 3145732
  29.8 20.8 %collective-permute-start.5 = (bf16[64,2048]{1,0:T(8,128)(2,1)S(1)}, bf16[64,2048]{1,0:T(8,128)(2,1)S(1)}, u32[]{:S(2)}, u32[]{:S(2)}) collective-permute-start(bf16[64,2048]{1,0:T(8,128)(2,1)S(1)} %get-tuple-element.34.refs_0_), channel_id=1, source_target_pairs={{0,32},{4,36},{8,40},{12,44},{16,48},{20,52},{24,56},{28,60},{32,6... | collective-permute-start | bytes 786440 | tf_op jit(solution)/shard_map/ppermute | solution.py:41
  36.9 15.2 %collective-permute-start.6 = (bf16[64,2048]{1,0:T(8,128)(2,1)S(1)}, bf16[64,2048]{1,0:T(8,128)(2,1)S(1)}, u32[]{:S(2)}, u32[]{:S(2)}) collective-permute-start(bf16[64,2048]{1,0:T(8,128)(2,1)S(1)} %get-tuple-element.34.refs_0_), channel_id=1, source_target_pairs={{0,64},{4,68},{8,72},{12,76},{16,80},{20,84},{24,88},{28,92},{32,9... | collective-permute-start | bytes 786440 | tf_op jit(solution)/shard_map/ppermute | solution.py:41
  48.1 19.3 %collective-permute-start.15 = (bf16[1024,256]{1,0:T(8,128)(2,1)S(1)}, bf16[1024,256]{1,0:T(8,128)(2,1)S(1)}, u32[]{:S(2)}, u32[]{:S(2)}) collective-permute-start(bf16[1024,256]{1,0:T(8,128)(2,1)S(1)} %collective-permute-done.13.refs_6_.refs_4_), channel_id=1, source_target_pairs={{0,4},{4,0},{8,12},{12,8},{16,20},{20,16},{24,28},{28,24},{32,36},... | collective-permute-start | bytes 1572872 | tf_op jit(solution)/shard_map/ppermute | solution.py:41
  49.0 7.9 %collective-permute-start.7 = (bf16[64,2048]{1,0:T(8,128)(2,1)S(1)}, bf16[64,2048]{1,0:T(8,128)(2,1)S(1)}, u32[]{:S(2)}, u32[]{:S(2)}) collective-permute-start(bf16[64,2048]{1,0:T(8,128)(2,1)S(1)} %get-tuple-element.34.refs_0_), channel_id=1, source_target_pairs={{0,96},{4,100},{8,104},{12,108},{16,112},{20,116},{24,120},{28,124... | collective-permute-start | bytes 786440 | tf_op jit(solution)/shard_map/ppermute | solution.py:41
  50.3 14.4 %collective-permute-start.10 = (bf16[64,2048]{1,0:T(8,128)(2,1)S(1)}, bf16[64,2048]{1,0:T(8,128)(2,1)S(1)}, u32[]{:S(2)}, u32[]{:S(2)}) collective-permute-start(bf16[64,2048]{1,0:T(8,128)(2,1)S(1)} %get-tuple-element.37.refs_0_.refs_4_), channel_id=1, source_target_pairs={{0,32},{4,36},{8,40},{12,44},{16,48},{20,52},{24,56},{28,60},{32,6... | collective-permute-start | bytes 786440 | tf_op jit(solution)/shard_map/ppermute | solution.py:41
  50.5 14.2 %collective-permute-start.11 = (bf16[64,2048]{1,0:T(8,128)(2,1)S(1)}, bf16[64,2048]{1,0:T(8,128)(2,1)S(1)}, u32[]{:S(2)}, u32[]{:S(2)}) collective-permute-start(bf16[64,2048]{1,0:T(8,128)(2,1)S(1)} %get-tuple-element.37.refs_0_.refs_4_), channel_id=1, source_target_pairs={{0,64},{4,68},{8,72},{12,76},{16,80},{20,84},{24,88},{28,92},{32,9... | collective-permute-start | bytes 786440 | tf_op jit(solution)/shard_map/ppermute | solution.py:41
  52.0 17.1 %collective-permute-start.16 = (bf16[1024,256]{1,0:T(8,128)(2,1)S(1)}, bf16[1024,256]{1,0:T(8,128)(2,1)S(1)}, u32[]{:S(2)}, u32[]{:S(2)}) collective-permute-start(bf16[1024,256]{1,0:T(8,128)(2,1)S(1)} %collective-permute-done.14.refs_7_.refs_5_), channel_id=1, source_target_pairs={{0,4},{4,0},{8,12},{12,8},{16,20},{20,16},{24,28},{28,24},{32,36},... | collective-permute-start | bytes 1572872 | tf_op jit(solution)/shard_map/ppermute | solution.py:41
  56.9 32.4 %collective-permute-start.8 = (bf16[2048,256]{1,0:T(8,128)(2,1)S(1)}, bf16[2048,256]{1,0:T(8,128)(2,1)S(1)}, u32[]{:S(2)}, u32[]{:S(2)}) collective-permute-start(bf16[2048,256]{1,0:T(8,128)(2,1)S(1)} %copy-done), channel_id=1, source_target_pairs={{0,4},{4,0},{8,12},{12,8},{16,20},{20,16},{24,28},{28,24},{32,36},... | collective-permute-start | bytes 3145736 | tf_op jit(solution)/shard_map/ppermute | solution.py:41
  64.7 13.6 %collective-permute-start.27 = (bf16[1024,256]{1,0:T(8,128)(2,1)S(1)}, bf16[1024,256]{1,0:T(8,128)(2,1)S(1)}, u32[]{:S(2)}, u32[]{:S(2)}) collective-permute-start(bf16[1024,256]{1,0:T(8,128)(2,1)S(1)} %collective-permute-done.13.refs_6_.refs_4_), channel_id=1, source_target_pairs={{0,8},{4,12},{8,16},{12,20},{16,24},{20,28},{24,0},{28,4},{32,40},... | collective-permute-start | bytes 1572872 | tf_op jit(solution)/shard_map/ppermute | solution.py:41
  64.7 15.5 %collective-permute-start.28 = (bf16[1024,256]{1,0:T(8,128)(2,1)S(1)}, bf16[1024,256]{1,0:T(8,128)(2,1)S(1)}, u32[]{:S(2)}, u32[]{:S(2)}) collective-permute-start(bf16[1024,256]{1,0:T(8,128)(2,1)S(1)} %collective-permute-done.18.refs_11_.refs_9_), channel_id=1, source_target_pairs={{0,24},{4,28},{8,0},{12,4},{16,8},{20,12},{24,16},{28,20},{32,56},... | collective-permute-start | bytes 1572872 | tf_op jit(solution)/shard_map/ppermute | solution.py:41
  67.4 12.9 %collective-permute-start.19 = (bf16[1024,256]{1,0:T(8,128)(2,1)S(1)}, bf16[1024,256]{1,0:T(8,128)(2,1)S(1)}, u32[]{:S(2)}, u32[]{:S(2)}) collective-permute-start(bf16[1024,256]{1,0:T(8,128)(2,1)S(1)} %collective-permute-done.17.refs_10_.refs_8_), channel_id=1, source_target_pairs={{0,4},{4,0},{8,12},{12,8},{16,20},{20,16},{24,28},{28,24},{32,36},... | collective-permute-start | bytes 1572872 | tf_op jit(solution)/shard_map/ppermute | solution.py:41
  69.1 11.4 %collective-permute-start.20 = (bf16[1024,256]{1,0:T(8,128)(2,1)S(1)}, bf16[1024,256]{1,0:T(8,128)(2,1)S(1)}, u32[]{:S(2)}, u32[]{:S(2)}) collective-permute-start(bf16[1024,256]{1,0:T(8,128)(2,1)S(1)} %collective-permute-done.18.refs_11_.refs_9_), channel_id=1, source_target_pairs={{0,4},{4,0},{8,12},{12,8},{16,20},{20,16},{24,28},{28,24},{32,36},... | collective-permute-start | bytes 1572872 | tf_op jit(solution)/shard_map/ppermute | solution.py:41
  78.3 14.4 %collective-permute-start.29 = (bf16[1024,256]{1,0:T(8,128)(2,1)S(1)}, bf16[1024,256]{1,0:T(8,128)(2,1)S(1)}, u32[]{:S(2)}, u32[]{:S(2)}) collective-permute-start(bf16[1024,256]{1,0:T(8,128)(2,1)S(1)} %collective-permute-done.27.refs_8_), channel_id=1, source_target_pairs={{0,4},{4,0},{8,12},{12,8},{16,20},{20,16},{24,28},{28,24},{32,36},... | collective-permute-start | bytes 1572872 | tf_op jit(solution)/shard_map/ppermute | solution.py:41
  80.3 14.1 %collective-permute-start.30 = (bf16[1024,256]{1,0:T(8,128)(2,1)S(1)}, bf16[1024,256]{1,0:T(8,128)(2,1)S(1)}, u32[]{:S(2)}, u32[]{:S(2)}) collective-permute-start(bf16[1024,256]{1,0:T(8,128)(2,1)S(1)} %collective-permute-done.28.refs_9_), channel_id=1, source_target_pairs={{0,4},{4,0},{8,12},{12,8},{16,20},{20,16},{24,28},{28,24},{32,36},... | collective-permute-start | bytes 1572872 | tf_op jit(solution)/shard_map/ppermute | solution.py:41
  80.3 7.5 %collective-permute-start.12 = (bf16[64,2048]{1,0:T(8,128)(2,1)S(1)}, bf16[64,2048]{1,0:T(8,128)(2,1)S(1)}, u32[]{:S(2)}, u32[]{:S(2)}) collective-permute-start(bf16[64,2048]{1,0:T(8,128)(2,1)S(1)} %get-tuple-element.37.refs_0_.refs_4_), channel_id=1, source_target_pairs={{0,96},{4,100},{8,104},{12,108},{16,112},{20,116},{24,120},{28,124... | collective-permute-start | bytes 786440 | tf_op jit(solution)/shard_map/ppermute | solution.py:41
  80.5 15.6 %collective-permute-start.35 = (bf16[2,256,256]{2,1,0:T(8,128)(2,1)S(1)}, bf16[2,256,256]{2,1,0:T(8,128)(2,1)S(1)}, u32[]{:S(2)}, u32[]{:S(2)}) collective-permute-start(bf16[2,256,256]{2,1,0:T(8,128)(2,1)S(1)} %get-tuple-element.52), channel_id=1, source_target_pairs={{0,8},{4,12},{8,16},{12,20},{16,24},{20,28},{24,0},{28,4},{32,40},... | collective-permute-start | bytes 786440 | tf_op jit(solution)/shard_map/ppermute | solution.py:41
  87.8 9.6 %collective-permute-start.36 = (bf16[2,256,256]{2,1,0:T(8,128)(2,1)S(1)}, bf16[2,256,256]{2,1,0:T(8,128)(2,1)S(1)}, u32[]{:S(2)}, u32[]{:S(2)}) collective-permute-start(bf16[2,256,256]{2,1,0:T(8,128)(2,1)S(1)} %get-tuple-element.53), channel_id=1, source_target_pairs={{0,16},{4,20},{8,24},{12,28},{16,0},{20,4},{24,8},{28,12},{32,48},... | collective-permute-start | bytes 786440 | tf_op jit(solution)/shard_map/ppermute | solution.py:41
  89.3 13.3 %collective-permute-start.37 = (bf16[2,256,256]{2,1,0:T(8,128)(2,1)S(1)}, bf16[2,256,256]{2,1,0:T(8,128)(2,1)S(1)}, u32[]{:S(2)}, u32[]{:S(2)}) collective-permute-start(bf16[2,256,256]{2,1,0:T(8,128)(2,1)S(1)} %get-tuple-element.54), channel_id=1, source_target_pairs={{0,24},{4,28},{8,0},{12,4},{16,8},{20,12},{24,16},{28,20},{32,56},... | collective-permute-start | bytes 786440 | tf_op jit(solution)/shard_map/ppermute | solution.py:41
  92.7 23.4 %collective-permute-start.21 = (bf16[128,1536]{1,0:T(8,128)(2,1)S(1)}, bf16[128,1536]{1,0:T(8,128)(2,1)S(1)}, u32[]{:S(2)}, u32[]{:S(2)}) collective-permute-start(bf16[128,1536]{1,0:T(8,128)(2,1)S(1)} %get-tuple-element.39), channel_id=1, source_target_pairs={{0,128},{128,0},{1,129},{129,1},{2,130},{130,2},{3,131},{131,3},{4... | collective-permute-start | bytes 1179656 | tf_op jit(solution)/shard_map/ppermute | solution.py:476
  94.4 13.9 %collective-permute-start.22 = (bf16[128,1024]{1,0:T(8,128)(2,1)S(1)}, bf16[128,1024]{1,0:T(8,128)(2,1)S(1)}, u32[]{:S(2)}, u32[]{:S(2)}) collective-permute-start(bf16[128,1024]{1,0:T(8,128)(2,1)S(1)} %get-tuple-element.42), channel_id=1, source_target_pairs={{0,128},{128,0},{1,129},{129,1},{2,130},{130,2},{3,131},{131,3},{4... | collective-permute-start | bytes 786440 | tf_op jit(solution)/shard_map/ppermute | solution.py:476
  96.1 17.7 %collective-permute-start.31 = (bf16[256,512]{1,0:T(8,128)(2,1)S(1)}, bf16[256,512]{1,0:T(8,128)(2,1)S(1)}, u32[]{:S(2)}, u32[]{:S(2)}) collective-permute-start(bf16[256,512]{1,0:T(8,128)(2,1)S(1)} %get-tuple-element.48), channel_id=1, source_target_pairs={{0,128},{128,0},{1,129},{129,1},{2,130},{130,2},{3,131},{131,3},{4... | collective-permute-start | bytes 786440 | tf_op jit(solution)/shard_map/ppermute | solution.py:476
  102.7 27.3 %collective-permute-start.38 = (bf16[4,2,128,256]{3,2,1,0:T(8,128)(2,1)S(1)}, bf16[4,2,128,256]{3,2,1,0:T(8,128)(2,1)S(1)}, u32[]{:S(2)}, u32[]{:S(2)}) collective-permute-start(bf16[4,2,128,256]{3,2,1,0:T(8,128)(2,1)S(1)} %trade.1), channel_id=1, source_target_pairs={{0,4},{4,0},{8,12},{12,8},{16,20},{20,16},{24,28},{28,24},{32,36},... | collective-permute-start | bytes 1572872 | tf_op jit(solution)/shard_map/ppermute | solution.py:41
  105.2 11.5 %collective-permute-start.9 = (bf16[128,512]{1,0:T(8,128)(2,1)S(1)}, bf16[128,512]{1,0:T(8,128)(2,1)S(1)}, u32[]{:S(2)}, u32[]{:S(2)}) collective-permute-start(bf16[128,512]{1,0:T(8,128)(2,1)S(1)} %get-tuple-element.36), channel_id=1, source_target_pairs={{0,128},{128,0},{1,129},{129,1},{2,130},{130,2},{3,131},{131,3},{4... | collective-permute-start | bytes 393224 | tf_op jit(solution)/shard_map/ppermute | solution.py:476
  108.3 10.6 %collective-permute-start.23 = (bf16[2,128,256]{2,1,0:T(8,128)(2,1)S(1)}, bf16[2,128,256]{2,1,0:T(8,128)(2,1)S(1)}, u32[]{:S(2)}, u32[]{:S(2)}) collective-permute-start(bf16[2,128,256]{2,1,0:T(8,128)(2,1)S(1)} %get-tuple-element.43.refs_2_), channel_id=1, source_target_pairs={{0,24},{4,28},{8,0},{12,4},{16,8},{20,12},{24,16},{28,20},{32,56},... | collective-permute-start | bytes 393224 | tf_op jit(solution)/shard_map/ppermute | solution.py:41
  113.9 14.6 %collective-permute-start.32 = (bf16[2,256,256]{2,1,0:T(8,128)(2,1)S(1)}, bf16[2,256,256]{2,1,0:T(8,128)(2,1)S(1)}, u32[]{:S(2)}, u32[]{:S(2)}) collective-permute-start(bf16[2,256,256]{2,1,0:T(8,128)(2,1)S(1)} %combine.7.refs_0_), channel_id=1, source_target_pairs={{0,16},{4,20},{8,24},{12,28},{16,0},{20,4},{24,8},{28,12},{32,48},... | collective-permute-start | bytes 786440 | tf_op jit(solution)/shard_map/ppermute | solution.py:41
  116.1 6.9 %collective-permute-start.24 = (bf16[2,128,256]{2,1,0:T(8,128)(2,1)S(1)}, bf16[2,128,256]{2,1,0:T(8,128)(2,1)S(1)}, u32[]{:S(2)}, u32[]{:S(2)}) collective-permute-start(bf16[2,128,256]{2,1,0:T(8,128)(2,1)S(1)} %get-tuple-element.44.refs_4_), channel_id=1, source_target_pairs={{0,8},{4,12},{8,16},{12,20},{16,24},{20,28},{24,0},{28,4},{32,40},... | collective-permute-start | bytes 393224 | tf_op jit(solution)/shard_map/ppermute | solution.py:41
  116.7 11.9 %collective-permute-start.25 = (bf16[2,128,256]{2,1,0:T(8,128)(2,1)S(1)}, bf16[2,128,256]{2,1,0:T(8,128)(2,1)S(1)}, u32[]{:S(2)}, u32[]{:S(2)}) collective-permute-start(bf16[2,128,256]{2,1,0:T(8,128)(2,1)S(1)} %get-tuple-element.45.refs_3_), channel_id=1, source_target_pairs={{0,24},{4,28},{8,0},{12,4},{16,8},{20,12},{24,16},{28,20},{32,56},... | collective-permute-start | bytes 393224 | tf_op jit(solution)/shard_map/ppermute | solution.py:41
  118.9 9.6 %collective-permute-start.26 = (bf16[2,128,256]{2,1,0:T(8,128)(2,1)S(1)}, bf16[2,128,256]{2,1,0:T(8,128)(2,1)S(1)}, u32[]{:S(2)}, u32[]{:S(2)}) collective-permute-start(bf16[2,128,256]{2,1,0:T(8,128)(2,1)S(1)} %get-tuple-element.46.refs_5_), channel_id=1, source_target_pairs={{0,8},{4,12},{8,16},{12,20},{16,24},{20,28},{24,0},{28,4},{32,40},... | collective-permute-start | bytes 393224 | tf_op jit(solution)/shard_map/ppermute | solution.py:41
  123.0 12.9 %collective-permute-start.33 = (bf16[512,256]{1,0:T(8,128)(2,1)S(1)}, bf16[512,256]{1,0:T(8,128)(2,1)S(1)}, u32[]{:S(2)}, u32[]{:S(2)}) collective-permute-start(bf16[512,256]{1,0:T(8,128)(2,1)S(1)} %pack.2), channel_id=1, source_target_pairs={{0,4},{4,0},{8,12},{12,8},{16,20},{20,16},{24,28},{28,24},{32,36},... | collective-permute-start | bytes 786440 | tf_op jit(solution)/shard_map/ppermute | solution.py:41
  128.6 7.3 %collective-permute-start.34 = (bf16[512,256]{1,0:T(8,128)(2,1)S(1)}, bf16[512,256]{1,0:T(8,128)(2,1)S(1)}, u32[]{:S(2)}, u32[]{:S(2)}) collective-permute-start(bf16[512,256]{1,0:T(8,128)(2,1)S(1)} %pack.3), channel_id=1, source_target_pairs={{0,4},{4,0},{8,12},{12,8},{16,20},{20,16},{24,28},{28,24},{32,36},... | collective-permute-start | bytes 786440 | tf_op jit(solution)/shard_map/ppermute | solution.py:41
  130.3 6.4 %copy-start.7 = (s32[256]{0:T(256)S(1)}, s32[256]{0:T(256)}, u32[]{:S(2)}) copy-start(s32[256]{0:T(256)} %param.15) | copy-start | bytes 3076
  131.1 12.1 %all-to-all-start = ((f32[32,1,256]{2,1,0:T(1,128)}), f32[32,1,256]{2,1,0:T(1,128)S(1)}, u32[]{:S(2)}, u32[]{:S(2)}) async-start(f32[32,1,256]{2,1,0:T(1,128)} %squares.3), calls=%async_computation | async-start | bytes 65536 | tf_op jit(solution)/shard_map/all_to_all | solution.py:498
  135.9 0.7 copy-start.3
  136.6 0.7 copy-start.6
  137.3 0.9 copy-start.4
